TPU v7x, 32 devices: a whole 2x2x4 slice. The times are simulated.
32 devices in a mesh: chan: 8 (over y, x, core), stn: 4 (over z).
Axes of the slice: x: 2, y: 2, z: 4, core: 2. Of those that a mesh axis runs over, the one named last changes fastest.
Arguments:
- measured_correlation: float32 [8, 8, 4096], P('chan', None, 'stn'), may hold values from -3 to 3
- model_correlation: float32 [8, 8, 16, 4096], P('chan', None, None, 'stn'), may hold values from -1.0606601 to 1.0606601
- source_pointing: int32 [16, 1], replicated, may hold values from 0 to 7
- antenna_pairs: int32 [2, 4096], P(None, 'stn'), may hold values from 0 to 511, as said below
- starting_jones_matrices: float32 [8, 8, 8, 512], P('chan'), may hold values from -1 to 2
- starting_polynomial_terms: float32 [3, 8, 8, 512], replicated, may hold values from -1 to 2
- starting_lagrange_scaled: float32 [8, 8, 8, 512], P('chan'), may hold values from -1.5 to 1.5
- augmented_lagrange_rhos: float32 [8], replicated, may hold values from 0.5 to 4
Outputs:
- solved_gains: float32 [8, 8, 8, 512], P('chan', None, None, 'stn')
- solved_dual: float32 [8, 8, 8, 512], P('chan', None, None, 'stn')
- fit_coeffs: float32 [3, 8, 8, 512], P(None, None, None, 'stn')
Inputs may be any that keep to these rules, and one draw needn't show every extreme that they name: `antenna_pairs`: row 0 holds a baseline's first station and row 1 its second, which differs from the first. The first station of every baseline in the i-th aligned block of 1024 baselines lies among stations i * 128 to (i + 1) * 128 - 1. `source_pointing`: every direction holds at least one component.
All inputs are finite; a program needn't handle non-finite values.
Results may differ from a plain program's by a relative error of at most 0.0001.
Values sent between devices are 32-bit elements; how exact they have to be, the bound alone decides.
No kernel may reach another device: no remote copies, remote signals or barrier semaphores. Data moves between devices by JAX's collectives and lax.ppermute only.
A program may use at most 64 MiB of HBM per device.

v0:
```python
from functools import partial

import jax
import jax.numpy as jnp
from jax import lax
from jax.sharding import PartitionSpec as P

CALIB_PATHS = 8
TERMS = 3
STEPS = 2
INNER = 2


student_nu = 2.0
squared_tolerance = 1e-06
highest = lax.Precision.HIGHEST


def entries(stacked):
    return [(stacked[slot_idx], stacked[4 + slot_idx]) for slot_idx in range(4)]


def assemble(matrix):
    return jnp.stack(
        [matrix[slot_idx][0] for slot_idx in range(4)]
        + [matrix[slot_idx][1] for slot_idx in range(4)],
        axis=0,
    )


def flatten(matrix):
    return [matrix[slot_idx][0] for slot_idx in range(4)] + [
        matrix[slot_idx][1] for slot_idx in range(4)
    ]


def multiply_pair(first_pair, second_pair):
    return (
        first_pair[0] * second_pair[0] - first_pair[1] * second_pair[1],
        first_pair[0] * second_pair[1] + first_pair[1] * second_pair[0],
    )


def add_pair(first_pair, second_pair):
    return (first_pair[0] + second_pair[0], first_pair[1] + second_pair[1])


def conjugate(value_pair):
    return (value_pair[0], -value_pair[1])


def matrix_product(factor_one, factor_two):
    return [
        add_pair(
            multiply_pair(factor_one[0], factor_two[0]), multiply_pair(factor_one[1], factor_two[2])
        ),
        add_pair(
            multiply_pair(factor_one[0], factor_two[1]), multiply_pair(factor_one[1], factor_two[3])
        ),
        add_pair(
            multiply_pair(factor_one[2], factor_two[0]), multiply_pair(factor_one[3], factor_two[2])
        ),
        add_pair(
            multiply_pair(factor_one[2], factor_two[1]), multiply_pair(factor_one[3], factor_two[3])
        ),
    ]


def adjoint(matrix):
    return [conjugate(matrix[0]), conjugate(matrix[2]), conjugate(matrix[1]), conjugate(matrix[3])]


def gram_parts(matrix):
    upper_sum = (
        matrix[0][0] * matrix[0][0]
        + matrix[0][1] * matrix[0][1]
        + matrix[1][0] * matrix[1][0]
        + matrix[1][1] * matrix[1][1]
    )
    lower_sum = (
        matrix[2][0] * matrix[2][0]
        + matrix[2][1] * matrix[2][1]
        + matrix[3][0] * matrix[3][0]
        + matrix[3][1] * matrix[3][1]
    )
    cross_term = add_pair(
        multiply_pair(matrix[0], conjugate(matrix[2])),
        multiply_pair(matrix[1], conjugate(matrix[3])),
    )
    return [upper_sum, lower_sum, cross_term[0], cross_term[1]]


def basis_table(channel_count):
    frequency = (2.0 * jnp.arange(channel_count, dtype=jnp.float32) + 1.0) / channel_count - 1.0
    columns = []
    for degree in range(TERMS):
        column = frequency**degree
        for earlier in columns:
            column = column - jnp.sum(earlier * column) / channel_count * earlier
        column = column / jnp.sqrt(jnp.sum(column * column) / channel_count)
        columns.append(column)
    return jnp.stack(columns, axis=1)


def combine_sources(cohere_f, source_pointing):
    member = (
        source_pointing[:, 0][:, None] == jnp.arange(CALIB_PATHS, dtype=jnp.int32)[None, :]
    ).astype(jnp.float32)
    return jnp.einsum("csb,sk->ckb", cohere_f, member, precision=highest)


def channel_state(vis_f, cohere_dir, spectral_jones_matrices, antenna_pairs):
    coherent = entries(cohere_dir)
    first_gain = entries(spectral_jones_matrices[:, :, antenna_pairs[0]])
    second_gain = entries(spectral_jones_matrices[:, :, antenna_pairs[1]])
    toward_first = matrix_product(coherent, adjoint(second_gain))
    own_terms = matrix_product(first_gain, toward_first)
    observed = entries(vis_f)
    residual = [
        (
            observed[slot_idx][0] - jnp.sum(own_terms[slot_idx][0], axis=0),
            observed[slot_idx][1] - jnp.sum(own_terms[slot_idx][1], axis=0),
        )
        for slot_idx in range(4)
    ]
    energy = residual[0][0] * residual[0][0] + residual[0][1] * residual[0][1]
    for slot_idx in range(1, 4):
        energy = (
            energy
            + residual[slot_idx][0] * residual[slot_idx][0]
            + residual[slot_idx][1] * residual[slot_idx][1]
        )
    return (residual, own_terms, toward_first, first_gain, coherent, energy)


def channel_sums(chan_state, weight, first_table, second_table, block_start):
    residual, own_terms, toward_first, first_gain, coherent, energy = chan_state
    target = [
        add_pair((residual[slot_idx][0][None], residual[slot_idx][1][None]), own_terms[slot_idx])
        for slot_idx in range(4)
    ]
    back_terms = matrix_product(first_gain, coherent)
    first_parts = (
        jnp.stack(
            gram_parts(toward_first) + flatten(matrix_product(target, adjoint(toward_first))),
            axis=0,
        )
        * weight
    )
    second_parts = (
        jnp.stack(
            gram_parts(adjoint(back_terms)) + flatten(matrix_product(adjoint(target), back_terms)),
            axis=0,
        )
        * weight
    )
    first_block = jnp.einsum("pkb,bs->pks", first_parts, first_table, precision=highest)
    every_station = jnp.einsum("pkb,bs->pks", second_parts, second_table, precision=highest)
    block_width = first_table.shape[1]
    own_rows = lax.dynamic_slice_in_dim(every_station, block_start, block_width, 2) + first_block
    return lax.dynamic_update_slice_in_dim(every_station, own_rows, block_start, 2)


def jones_estimator(
    least_squares_equations, pivot_spectral_point, spectral_jones_matrices, augmented_lagrange_rhos
):
    augmented_rho_factor = augmented_lagrange_rhos[:, None]
    diag_one = least_squares_equations[0] + augmented_rho_factor
    diag_two = least_squares_equations[1] + augmented_rho_factor
    determinant = (
        diag_one * diag_two
        - least_squares_equations[2] * least_squares_equations[2]
        - least_squares_equations[3] * least_squares_equations[3]
    )
    zero_part = jnp.zeros_like(determinant)
    inverse = [
        (diag_two / determinant, zero_part),
        (-least_squares_equations[2] / determinant, -least_squares_equations[3] / determinant),
        (-least_squares_equations[2] / determinant, least_squares_equations[3] / determinant),
        (diag_one / determinant, zero_part),
    ]
    right_side = entries(
        least_squares_equations[4:] + augmented_rho_factor[None] * pivot_spectral_point
    )
    solution = assemble(matrix_product(right_side, inverse))
    return 0.5 * (spectral_jones_matrices + solution)


def body(
    measured_correlation,
    model_correlation,
    source_pointing,
    antenna_pairs,
    starting_jones_matrices,
    starting_polynomial_terms,
    starting_lagrange_scaled,
    augmented_lagrange_rhos,
):
    local_ch = measured_correlation.shape[0]
    stations = starting_jones_matrices.shape[3]
    block_size = stations // lax.axis_size("stn")
    block_start = lax.axis_index("stn") * block_size
    total_ch = local_ch * lax.axis_size("chan")
    sample_count = total_ch * measured_correlation.shape[2] * lax.axis_size("stn")
    my_basis = lax.dynamic_slice_in_dim(
        basis_table(total_ch), lax.axis_index("chan") * local_ch, local_ch, 0
    )
    cohere_dir = jax.vmap(combine_sources, (0, None))(model_correlation, source_pointing)
    first_table = (
        (antenna_pairs[0] - block_start)[:, None]
        == jnp.arange(block_size, dtype=jnp.int32)[None, :]
    ).astype(jnp.float32)
    second_table = (
        antenna_pairs[1][:, None] == jnp.arange(stations, dtype=jnp.int32)[None, :]
    ).astype(jnp.float32)
    state_fn = jax.vmap(channel_state, (0, 0, 0, None))
    sums_fn = jax.vmap(
        partial(
            channel_sums,
            first_table=first_table,
            second_table=second_table,
            block_start=block_start,
        ),
        (0, 0),
    )
    estimate_routine = jax.vmap(jones_estimator, (0, 0, 0, None))

    def own_block(array):
        return lax.dynamic_slice_in_dim(array, block_start, block_size, 3)

    consensus = jnp.einsum("ft,tcks->fcks", my_basis, starting_polynomial_terms, precision=highest)
    whole_jones_matrix = starting_jones_matrices
    dual_now = starting_lagrange_scaled
    gain_mine = starting_jones_matrices
    pending = None
    fit_now = starting_polynomial_terms
    for step_idx in range(STEPS):
        pivot_antenna = consensus - dual_now
        for inner_idx in range(INNER):
            chan_state = state_fn(
                measured_correlation, cohere_dir, whole_jones_matrix, antenna_pairs
            )
            mean_square = (
                lax.psum(jnp.sum(chan_state[5]), ("chan", "stn")) / sample_count + squared_tolerance
            )
            weight = (student_nu + 2.0) / (student_nu + chan_state[5] / mean_square)
            least_squares_equations = sums_fn(chan_state, weight)
            whole_accumulated_totals = lax.psum(least_squares_equations, "stn")
            whole_jones_matrix = estimate_routine(
                whole_accumulated_totals, pivot_antenna, whole_jones_matrix, augmented_lagrange_rhos
            )
            gain_mine = whole_jones_matrix
        partial_fit = jnp.einsum("ft,fcks->tcks", my_basis, gain_mine + dual_now, precision=highest)
        fit_now = lax.psum(partial_fit, "chan") / total_ch
        consensus = jnp.einsum("ft,tcks->fcks", my_basis, fit_now, precision=highest)
        dual_now = dual_now + gain_mine - consensus
    return (own_block(gain_mine), own_block(dual_now), own_block(fit_now))


def solution(mesh):
    placed = (
        P("chan", None, "stn"),
        P("chan", None, None, "stn"),
        P(),
        P(None, "stn"),
        P("chan", None, None, None),
        P(),
        P("chan", None, None, None),
        P(),
    )
    return jax.shard_map(
        body,
        mesh=mesh,
        in_specs=placed,
        out_specs=(
            P("chan", None, None, "stn"),
            P("chan", None, None, "stn"),
            P(None, None, None, "stn"),
        ),
        check_vma=False,
    )
```

profile of v0, /device:TPU:0, one launch (start us, length us, event | category | flops | bytes accessed | tf_op | source)
XLA Modules:
  0.0 534.8 jit_solution(3968500334893282561)
XLA Ops:
  10.2 1.0 fusion.296
  11.2 1.7 copy.196
  12.9 9.1 %gather_fusion.1 = f32[1024,8,8]{2,1,0:T(8,128)} fusion(f32[8,8,512]{1,0,2:T(8,128)S(1)} %bitcast.987, s32[1024]{0:T(1024)S(1)} %get-tuple-element.362), kind=kCustom, calls=%fused_computation.1 | custom fusion | bytes 528384 | tf_op jit(solution)/shard_map/vmap()/gather | solution.py:115
  21.9 2.8 copy.209
  24.7 9.1 %gather_fusion = f32[1024,8,8]{2,1,0:T(8,128)} fusion(f32[8,8,512]{1,0,2:T(8,128)S(1)} %bitcast.988, s32[1024]{0:T(1024)S(1)} %get-tuple-element.363), kind=kCustom, calls=%fused_computation | custom fusion | bytes 528384 | tf_op jit(solution)/shard_map/vmap()/gather | solution.py:114
  33.8 2.8 copy.197
  38.6 42.2 %psum.70 = f32[]{:T(128)} all-reduce(f32[]{:T(128)} %fusion.207), channel_id=1, replica_groups=mesh['chan'=8,'stn'=4] {'chan','stn'}, use_global_device_ids=true, to_apply=%region_9.0 | all-reduce | flops 1 | bytes 8 | tf_op jit(solution)/shard_map/psum | solution.py:244
  82.9 1.9 fusion.7
  84.9 2.3 fusion.16
  87.2 1.0 scatter.14
  95.5 1.2 fusion.27
  96.7 27.4 %all-reduce.8.cloned.1.call-done = f32[1,12,8,512]{3,2,1,0:T(8,128)} async-done(((f32[1,12,8,512]{3,2,1,0:T(8,128)}), f32[1,12,8,512]{3,2,1,0:T(8,128)}) %all-reduce.8.cloned.1.call-update) | async-done | bytes 196624 | tf_op jit(solution)/shard_map/psum | solution.py:248
  124.0 1.0 slice_add_fusion.3
  127.5 1.7 copy.236
  129.1 9.1 %gather_fusion.3 = f32[1024,8,8]{2,1,0:T(8,128)} fusion(f32[8,8,512]{1,0,2:T(8,128)S(1)} %copy.236, s32[1024]{0:T(1024)S(1)} %get-tuple-element.362), kind=kCustom, calls=%fused_computation.3 | custom fusion | bytes 528384 | tf_op jit(solution)/shard_map/vmap()/gather | solution.py:115
  138.2 9.1 %gather_fusion.2 = f32[1024,8,8]{2,1,0:T(8,128)} fusion(f32[8,8,512]{1,0,2:T(8,128)S(1)} %copy.236, s32[1024]{0:T(1024)S(1)} %get-tuple-element.363), kind=kCustom, calls=%fused_computation.2 | custom fusion | bytes 528384 | tf_op jit(solution)/shard_map/vmap()/gather | solution.py:114
  147.3 2.8 copy.243
  150.2 2.8 copy.237
  153.9 40.5 %psum.72 = f32[]{:T(128)} all-reduce(f32[]{:T(128)} %fusion.206), channel_id=1, replica_groups=mesh['chan'=8,'stn'=4] {'chan','stn'}, use_global_device_ids=true, to_apply=%region_26.0 | all-reduce | flops 1 | bytes 8 | tf_op jit(solution)/shard_map/psum | solution.py:244
  195.8 1.0 fusion.5
  196.8 2.3 fusion.14
  199.1 1.0 scatter.15
  200.9 34.9 %all-reduce.10.cloned.1.call-done = f32[1,12,8,512]{3,2,0,1:T(8,128)} async-done(((f32[1,12,8,512]{3,2,0,1:T(8,128)}), f32[1,12,8,512]{3,2,0,1:T(8,128)}) %all-reduce.10.cloned.1.call-update) | async-done | bytes 196624 | tf_op jit(solution)/shard_map/psum | solution.py:248
  235.8 1.0 slice_add_fusion.2
  239.4 9.1 %gather_fusion.5 = f32[1024,8,8]{2,1,0:T(8,128)} fusion(f32[8,8,512]{1,0,2:T(8,128)S(1)} %copy.249, s32[1024]{0:T(1024)S(1)} %get-tuple-element.362), kind=kCustom, calls=%fused_computation.5 | custom fusion | bytes 528384 | tf_op jit(solution)/shard_map/vmap()/gather | solution.py:115
  248.5 9.1 %gather_fusion.4 = f32[1024,8,8]{2,1,0:T(8,128)} fusion(f32[8,8,512]{1,0,2:T(8,128)S(1)} %copy.249, s32[1024]{0:T(1024)S(1)} %get-tuple-element.363), kind=kCustom, calls=%fused_computation.4 | custom fusion | bytes 528384 | tf_op jit(solution)/shard_map/vmap()/gather | solution.py:114
  257.5 2.8 copy.256
  260.5 2.8 copy.250
  265.1 40.3 %psum.74 = f32[]{:T(128)} all-reduce(f32[]{:T(128)} %fusion.205), channel_id=1, replica_groups=mesh['chan'=8,'stn'=4] {'chan','stn'}, use_global_device_ids=true, to_apply=%region_37.0 | all-reduce | flops 1 | bytes 8 | tf_op jit(solution)/shard_map/psum | solution.py:244
  307.8 2.3 fusion.12
  310.1 1.0 scatter.16
  312.1 7.3 %all-reduce.14.cloned.1.call-done = f32[3,8,8,512]{3,2,1,0:T(8,128)} async-done(((f32[3,8,8,512]{3,2,1,0:T(8,128)}), f32[3,8,8,512]{3,2,1,0:T(8,128)}) %all-reduce.14.cloned.1.call-update) | async-done | bytes 393232 | tf_op jit(solution)/shard_map/psum | solution.py:254
  319.3 1.0 broadcast_multiply_fusion.2
  320.3 1.2 fusion.25
  321.5 34.4 %all-reduce.12.cloned.1.call-done = f32[1,12,8,512]{3,2,0,1:T(8,128)} async-done(((f32[1,12,8,512]{3,2,0,1:T(8,128)}), f32[1,12,8,512]{3,2,0,1:T(8,128)}) %all-reduce.12.cloned.1.call-update) | async-done | bytes 196624 | tf_op jit(solution)/shard_map/psum | solution.py:248
  355.9 1.0 slice_add_fusion.1
  360.0 9.1 %gather_fusion.7 = f32[1024,8,8]{2,1,0:T(8,128)} fusion(f32[8,8,512]{1,0,2:T(8,128)S(1)} %copy.264, s32[1024]{0:T(1024)S(1)} %get-tuple-element.362), kind=kCustom, calls=%fused_computation.7 | custom fusion | bytes 528384 | tf_op jit(solution)/shard_map/vmap()/gather | solution.py:115
  369.2 9.1 %gather_fusion.6 = f32[1024,8,8]{2,1,0:T(8,128)} fusion(f32[8,8,512]{1,0,2:T(8,128)S(1)} %copy.264, s32[1024]{0:T(1024)S(1)} %get-tuple-element.363), kind=kCustom, calls=%fused_computation.6 | custom fusion | bytes 528384 | tf_op jit(solution)/shard_map/vmap()/gather | solution.py:114
  378.2 2.8 copy.271
  381.1 2.8 copy.265
  384.9 40.3 %psum.77 = f32[]{:T(128)} all-reduce(f32[]{:T(128)} %fusion.204), channel_id=1, replica_groups=mesh['chan'=8,'stn'=4] {'chan','stn'}, use_global_device_ids=true, to_apply=%region_49.0 | all-reduce | flops 1 | bytes 8 | tf_op jit(solution)/shard_map/psum | solution.py:244
  427.5 2.3 fusion.10
  429.9 1.0 scatter.19
  431.6 34.9 %all-reduce.16.cloned.1.call-done = f32[1,12,8,512]{3,2,0,1:T(8,128)} async-done(((f32[1,12,8,512]{3,2,0,1:T(8,128)}), f32[1,12,8,512]{3,2,0,1:T(8,128)}) %all-reduce.16.cloned.1.call-update) | async-done | bytes 196624 | tf_op jit(solution)/shard_map/psum | solution.py:248
  466.5 1.0 slice_add_fusion
  470.9 53.6 %all-reduce.18.cloned.1.call-done = f32[3,8,8,512]{3,2,1,0:T(8,128)} async-done(((f32[3,8,8,512]{3,2,1,0:T(8,128)}), f32[3,8,8,512]{3,2,1,0:T(8,128)}) %all-reduce.18.cloned.1.call-update) | async-done | bytes 393232 | tf_op jit(solution)/shard_map/psum | solution.py:254
  524.5 1.0 broadcast_multiply_fusion.1
  526.2 1.1 fusion.23
  (229 shorter events, 33.0 us)
Async XLA Ops:
  7.2 29.5 %copy-start = (f32[1,8,16,1024]{3,2,1,0:T(8,128)S(1)}, f32[1,8,16,1024]{3,2,1,0:T(8,128)}, u32[]{:S(2)}) copy-start(f32[1,8,16,1024]{3,2,1,0:T(8,128)} %param.17) | copy-start | bytes 1572868
  7.2 116.8 %all-reduce.8.cloned.1.call-start = ((), (), s32[]{:S(2)}) async-start(), calls=%async_computation | async-start | bytes 393216 | tf_op jit(solution)/shard_map/psum | solution.py:248
  21.9 14.7 %copy-start.17 = (s32[16,1]{0,1:T(1,128)S(1)}, s32[16,1]{0,1:T(1,128)}, u32[]{:S(2)}) copy-start(s32[16,1]{0,1:T(1,128)} %param.18) | copy-start | bytes 196
  33.8 3.5 copy-start.1
  37.1 44.4 %copy-start.16 = (s32[4]{0:T(128)S(1)}, s32[4]{0:T(128)}, u32[]{:S(2)}) copy-start(s32[4]{0:T(128)} %constant.139.clone.1) | copy-start | bytes 52
  37.3 58.2 %copy-start.7 = (f32[3,8,8,512]{3,2,1,0:T(8,128)S(1)}, f32[3,8,8,512]{3,2,1,0:T(8,128)}, u32[]{:S(2)}) copy-start(f32[3,8,8,512]{3,2,1,0:T(8,128)} %param.21) | copy-start | bytes 1179652
  80.8 43.2 %copy-start.5 = (f32[1,8,8,512]{3,2,1,0:T(8,128)S(1)}, f32[1,8,8,512]{3,2,1,0:T(8,128)}, u32[]{:S(2)}) copy-start(f32[1,8,8,512]{3,2,1,0:T(8,128)} %param.22) | copy-start | bytes 393220
  80.8 43.2 %copy-start.14 = (f32[8]{0:T(128)S(1)}, f32[8]{0:T(128)}, u32[]{:S(2)}) copy-start(f32[8]{0:T(128)} %param.23) | copy-start | bytes 100
  81.1 45.7 %copy-start.6 = (f32[1,8,8,512]{3,2,1,0:T(8,128)S(1)}, f32[1,8,8,512]{3,2,1,0:T(8,128)}, u32[]{:S(2)}) copy-start(f32[1,8,8,512]{3,2,1,0:T(8,128)} %param.20) | copy-start | bytes 393220
  81.5 1.4 copy-start.15
  88.2 0.7 copy-start.12
  88.9 146.9 %all-reduce.10.cloned.1.call-start = ((), (), s32[]{:S(2)}) async-start(), calls=%async_computation.1 | async-start | bytes 393216 | tf_op jit(solution)/shard_map/psum | solution.py:248
  200.1 0.7 copy-start.13
  200.8 118.5 %all-reduce.14.cloned.1.call-start = ((), (), s32[]{:S(2)}) async-start(), calls=%async_computation.3 | async-start | bytes 786432 | tf_op jit(solution)/shard_map/psum | solution.py:254
  238.6 9.9 %copy-start.2 = (f32[1,8,8,512]{3,2,1,0:T(8,128)}, f32[1,8,8,512]{3,2,1,0:T(8,128)S(1)}, u32[]{:S(2)}) copy-start(f32[1,8,8,512]{3,2,1,0:T(8,128)S(1)} %get-tuple-element.150) | copy-start | bytes 393220
  265.0 90.8 %all-reduce.12.cloned.1.call-start = ((), (), s32[]{:S(2)}) async-start(), calls=%async_computation.2 | async-start | bytes 393216 | tf_op jit(solution)/shard_map/psum | solution.py:248
  306.4 52.8 %copy-start.3 = (f32[1,8,8,512]{3,2,1,0:T(8,128)S(1)}, f32[1,8,8,512]{3,2,1,0:T(8,128)}, u32[]{:S(2)}) copy-start(f32[1,8,8,512]{3,2,1,0:T(8,128)} %copy-done.2) | copy-start | bytes 393220
  311.1 0.7 copy-start.10
  311.8 154.7 %all-reduce.16.cloned.1.call-start = ((), (), s32[]{:S(2)}) async-start(), calls=%async_computation.4 | async-start | bytes 393216 | tf_op jit(solution)/shard_map/psum | solution.py:248
  358.6 0.6 copy-start.8
  426.0 43.3 %copy-start.4 = (f32[1,8,8,512]{3,2,1,0:T(8,128)S(1)}, f32[1,8,8,512]{3,2,1,0:T(8,128)}, u32[]{:S(2)}) copy-start(f32[1,8,8,512]{3,2,1,0:T(8,128)} %copy-done.2) | copy-start | bytes 393220
  426.0 43.3 %copy-start.9 = (f32[8,1,8,512]{3,2,0,1:T(8,128)S(1)}, f32[8,1,8,512]{3,2,0,1:T(8,128)}, u32[]{:S(2)}) copy-start(f32[8,1,8,512]{3,2,0,1:T(8,128)} %copy-done.8) | copy-start | bytes 393220
  430.9 0.7 copy-start.11
  431.6 92.9 %all-reduce.18.cloned.1.call-start = ((), (), s32[]{:S(2)}) async-start(), calls=%async_computation.5 | async-start | bytes 786432 | tf_op jit(solution)/shard_map/psum | solution.py:254
Sparse Core Ops, SparseCore 0:
  89.0 34.9 all-reduce.7
  200.9 34.8 all-reduce.9
  265.2 54.1 all-reduce.13
  321.5 34.3 all-reduce.11
  431.7 34.8 all-reduce.15
  470.4 54.0 all-reduce.17
where the time goes:
time: 538 us; the launch traced here: 535 us
  waiting for transfers between devices  192 us (36%)
  blocking collectives  163 us (30%)
  local copies, waits for them, and re-layouts  111 us (21%)
  other arithmetic  28.8 us (5%)
  between operations  21.2 us (4%)
  matrix products  17.9 us (3%)
    psum x4, blocking collectives, body(): lax.psum(jnp.sum(chan_state[5]), ('chan', 'stn')) / sample_count  163 us
    psum x4, waiting for transfers between devices, body(): whole_accumulated_totals = lax.psum(least_squares_equations, 'stn')  132 us
    psum x2, waiting for transfers between devices, body(): fit_now = lax.psum(partial_fit, 'chan') / total_ch  60.8 us
    gather x8, local copies, waits for them, and re-layouts, channel_state(): second_gain = entries(spectral_jones_matrices[:, :, antenna_pairs[1]])  47.6 us
    gather x8, local copies, waits for them, and re-layouts, channel_state(): first_gain = entries(spectral_jones_matrices[:, :, antenna_pairs[0]])  47.5 us
  transfers between devices with their start and end apart: 6, of which 6 were waited for; matrix products, arithmetic and copies ran while one was open for 2% of the time, Pallas kernels for 0%

commit v1 on v0

v1 whole, which is shorter than its diff:
```python
from functools import partial

import jax
import jax.numpy as jnp
from jax import lax
from jax.experimental import pallas as pl
from jax.experimental.pallas import tpu as pltpu
from jax.sharding import PartitionSpec as P

TERMS = 3
STEPS = 2
INNER = 2
COMPS = 8
LANES = 128

student_nu = 2.0
squared_tolerance = 1e-06
f32 = jnp.float32
bf16 = jnp.bfloat16


def cmul(a, b):
    return (a[0] * b[0] - a[1] * b[1], a[0] * b[1] + a[1] * b[0])


def cadd(a, b):
    return (a[0] + b[0], a[1] + b[1])


def conj(a):
    return (a[0], -a[1])


def mmul(a, b):
    return [
        cadd(cmul(a[0], b[0]), cmul(a[1], b[2])),
        cadd(cmul(a[0], b[1]), cmul(a[1], b[3])),
        cadd(cmul(a[2], b[0]), cmul(a[3], b[2])),
        cadd(cmul(a[2], b[1]), cmul(a[3], b[3])),
    ]


def adj(m):
    return [conj(m[0]), conj(m[2]), conj(m[1]), conj(m[3])]


def flat(m):
    return [m[i][0] for i in range(4)] + [m[i][1] for i in range(4)]


def square(a):
    return a[0] * a[0] + a[1] * a[1]


def gram(m):
    cross = cadd(cmul(m[0], conj(m[2])), cmul(m[1], conj(m[3])))
    return [
        square(m[0]) + square(m[1]),
        square(m[2]) + square(m[3]),
        cross[0],
        cross[1],
    ]


def basis_table(channel_count):
    frequency = (2.0 * jnp.arange(channel_count, dtype=f32) + 1.0) / channel_count - 1.0
    columns = []
    for degree in range(TERMS):
        column = frequency**degree
        for earlier in columns:
            column = column - jnp.sum(earlier * column) / channel_count * earlier
        column = column / jnp.sqrt(jnp.sum(column * column) / channel_count)
        columns.append(column)
    return jnp.stack(columns, axis=1)


def split(x):
    hi = x.astype(bf16)
    lo = (x - hi.astype(f32)).astype(bf16)
    return hi, lo


def load(ref, paths, lanes):
    rows = [ref[c * paths : (c + 1) * paths, lanes] for c in range(COMPS)]
    return [(rows[i], rows[4 + i]) for i in range(4)]


def combine_kernel(point_ref, model_ref, vis_ref, pair_ref, out_ref, *, paths, comps):
    width = out_ref.shape[1]
    which = lax.broadcasted_iota(jnp.int32, (paths, width), 0)
    for c in range(COMPS):
        total = jnp.zeros((paths, width), f32)
        for s in range(comps):
            row = model_ref[c * comps + s : c * comps + s + 1, :]
            total = total + jnp.where(which == point_ref[s], row, 0.0)
        out_ref[c * paths : (c + 1) * paths, :] = total
    base = COMPS * paths
    out_ref[base : base + COMPS, :] = vis_ref[...]
    out_ref[base + COMPS : base + COMPS + 2, :] = pair_ref[...].astype(f32)


class Plan:
    def __init__(self, paths, stations, blocks, width):
        self.paths, self.stations = paths, stations
        self.blocks, self.width = blocks, width
        self.rows = COMPS * paths
        own = stations // blocks
        self.own = own
        self.window = min(stations, max(own, LANES))
        self.starts = [i * own // self.window * self.window for i in range(blocks)]


def make_onehots(plan, msg_ref, ohp_ref, ohq_ref):
    width, base = plan.width, plan.rows + COMPS
    for i in range(plan.blocks):
        lanes = slice(i * width, (i + 1) * width)
        first = msg_ref[base : base + 1, lanes].astype(jnp.int32) - plan.starts[i]
        second = msg_ref[base + 1 : base + 2, lanes].astype(jnp.int32)
        pos = lax.broadcasted_iota(jnp.int32, (plan.window, width), 0)
        ohp_ref[:, lanes] = jnp.where(pos == first, 1.0, 0.0).astype(bf16)
        pos = lax.broadcasted_iota(jnp.int32, (plan.stations, width), 0)
        ohq_ref[:, lanes] = jnp.where(pos == second, 1.0, 0.0).astype(bf16)


def residuals(plan, gains, msg_ref, ohp_ref, ohq_ref, x_ref, y_ref, h_ref, e_ref, jp_ref, jq_ref):
    paths, rows, width = plan.paths, plan.rows, plan.width
    hi, lo = split(gains)
    both = jnp.concatenate([hi, lo], axis=0)
    total = jnp.zeros((1, LANES), f32)
    for i in range(plan.blocks):
        block = slice(i * width, (i + 1) * width)
        window = slice(plan.starts[i], plan.starts[i] + plan.window)
        got = jnp.dot(both, ohq_ref[:, block], preferred_element_type=f32)
        jq_ref[...] = got[:rows] + got[rows:]
        got = jnp.dot(both[:, window], ohp_ref[:, block], preferred_element_type=f32)
        jp_ref[...] = got[:rows] + got[rows:]

        def piece(t, carry):
            here = pl.ds(pl.multiple_of(t * LANES, LANES), LANES)
            there = pl.ds(pl.multiple_of(i * width + t * LANES, LANES), LANES)
            coherent = load(msg_ref, paths, there)
            y = mmul(coherent, adj(load(jq_ref, paths, here)))
            for c, v in enumerate(flat(y)):
                y_ref[c * paths : (c + 1) * paths, there] = v
            first = load(jp_ref, paths, here)
            g = flat(mmul(first, y))
            energy = jnp.zeros((1, LANES), f32)
            for c in range(COMPS):
                r = msg_ref[rows + c : rows + c + 1, there] - jnp.sum(g[c], axis=0, keepdims=True)
                energy = energy + r * r
                x_ref[c * paths : (c + 1) * paths, there] = r + g[c]
            for c, v in enumerate(flat(mmul(first, coherent))):
                h_ref[c * paths : (c + 1) * paths, there] = v
            e_ref[0:1, there] = energy
            return carry + energy

        total = lax.fori_loop(0, width // LANES, piece, total)
    return total


def normal_sums(plan, noise, ohp_ref, ohq_ref, x_ref, y_ref, h_ref, e_ref, fp_ref, sp_ref, acc_ref):
    paths, width = plan.paths, plan.width
    half = 12 * paths
    contract = (((1,), (1,)), ((), ()))
    for i in range(plan.blocks):
        block = slice(i * width, (i + 1) * width)
        window = slice(plan.starts[i], plan.starts[i] + plan.window)

        def piece(t, carry):
            here = pl.ds(pl.multiple_of(t * LANES, LANES), LANES)
            there = pl.ds(pl.multiple_of(i * width + t * LANES, LANES), LANES)
            weight = (student_nu + 2.0) / (student_nu + e_ref[0:1, there] / noise)
            weight = jnp.broadcast_to(weight, (paths, LANES))
            x = [(a * weight, b * weight) for a, b in load(x_ref, paths, there)]
            y = load(y_ref, paths, there)
            parts = [v * weight for v in gram(y)] + flat(mmul(x, adj(y)))
            hi, lo = split(jnp.concatenate(parts, axis=0))
            fp_ref[0:half, here] = hi
            fp_ref[half : 2 * half, here] = lo
            h = load(h_ref, paths, there)
            parts = [v * weight for v in gram(adj(h))] + flat(mmul(adj(x), h))
            hi, lo = split(jnp.concatenate(parts, axis=0))
            sp_ref[0:half, here] = hi
            sp_ref[half : 2 * half, here] = lo
            return carry

        lax.fori_loop(0, width // LANES, piece, 0)
        got = lax.dot_general(sp_ref[...], ohq_ref[:, block], contract, preferred_element_type=f32)
        got = got[:half] + got[half:]
        if i == 0:
            acc_ref[...] = got
        else:
            acc_ref[...] += got
        got = lax.dot_general(fp_ref[...], ohp_ref[:, block], contract, preferred_element_type=f32)
        acc_ref[:, window] += got[:half] + got[half:]


def solve(plan, acc_ref, anchor, gains, rho):
    paths = plan.paths
    part = [acc_ref[c * paths : (c + 1) * paths, :] for c in range(12)]
    a, d = part[0] + rho, part[1] + rho
    inv = 1.0 / (a * d - part[2] * part[2] - part[3] * part[3])
    a, d, c0, c1 = a * inv, d * inv, part[2] * inv, part[3] * inv
    rhs = [part[4 + c] + rho * anchor[c * paths : (c + 1) * paths] for c in range(COMPS)]
    out = [None] * COMPS
    for row in (0, 2):
        u = (rhs[row], rhs[4 + row])
        v = (rhs[row + 1], rhs[5 + row])
        left = cmul(v, (c0, -c1))
        right = cmul(u, (c0, c1))
        out[row], out[4 + row] = u[0] * d - left[0], u[1] * d - left[1]
        out[row + 1], out[5 + row] = v[0] * a - right[0], v[1] * a - right[1]
    return 0.5 * (gains + jnp.concatenate(out, axis=0))


def noise_of(energy, count):
    per_lane = jnp.sum(energy, axis=0, keepdims=True)
    return jnp.sum(per_lane, axis=1, keepdims=True) / count + squared_tolerance


def params(limit=24 << 20):
    return pltpu.CompilerParams(vmem_limit_bytes=limit)


VM = pl.BlockSpec(memory_space=pltpu.VMEM)
SM = pl.BlockSpec(memory_space=pltpu.SMEM)


def first_kernel(gain_ref, msg_ref, ohp_ref, ohq_ref, x_ref, y_ref, h_ref, e_ref, sum_ref,
                 jp_ref, jq_ref, *, plan):
    make_onehots(plan, msg_ref, ohp_ref, ohq_ref)
    total = residuals(plan, gain_ref[...], msg_ref, ohp_ref, ohq_ref, x_ref, y_ref, h_ref, e_ref,
                      jp_ref, jq_ref)
    sum_ref[...] = jnp.broadcast_to(total, sum_ref.shape)


def rho_column(rho_ref, paths, width):
    which = lax.broadcasted_iota(jnp.int32, (paths, width), 0)
    out = jnp.zeros((paths, width), f32)
    for k in range(paths):
        out = jnp.where(which == k, rho_ref[k], out)
    return out


def middle_kernel(rho_ref, gain_ref, anchor_ref, energy_ref, msg_ref, ohp_ref, ohq_ref,
                  x_ref, y_ref, h_ref, e_ref,
                  gain_out, x_out, y_out, h_out, e_out, sum_ref,
                  jp_ref, jq_ref, fp_ref, sp_ref, acc_ref, *, plan, count):
    noise = noise_of(energy_ref[...], count)
    normal_sums(plan, noise, ohp_ref, ohq_ref, x_ref, y_ref, h_ref, e_ref, fp_ref, sp_ref, acc_ref)
    rho = rho_column(rho_ref, plan.paths, plan.stations)
    gains = solve(plan, acc_ref, anchor_ref[...], gain_ref[...], rho)
    gain_out[...] = gains
    total = residuals(plan, gains, msg_ref, ohp_ref, ohq_ref, x_out, y_out, h_out, e_out,
                      jp_ref, jq_ref)
    sum_ref[...] = jnp.broadcast_to(total, sum_ref.shape)


def last_kernel(rho_ref, gain_ref, anchor_ref, energy_ref, ohp_ref, ohq_ref,
                x_ref, y_ref, h_ref, e_ref,
                gain_out, fp_ref, sp_ref, acc_ref, *, plan, count):
    noise = noise_of(energy_ref[...], count)
    normal_sums(plan, noise, ohp_ref, ohq_ref, x_ref, y_ref, h_ref, e_ref, fp_ref, sp_ref, acc_ref)
    rho = rho_column(rho_ref, plan.paths, plan.stations)
    gain_out[...] = solve(plan, acc_ref, anchor_ref[...], gain_ref[...], rho)


def body(vis, model, pointing, pairs, gains, poly, dual, rhos, *, chans, blocks):
    paths, stations = gains.shape[2], gains.shape[3]
    sources, width = model.shape[2], model.shape[3]
    rows = COMPS * paths
    total_base = blocks * width
    total_ch = vis.shape[0] * chans
    plan = Plan(paths, stations, blocks, width)
    count = float(total_ch * total_base)
    own = plan.own
    block_start = lax.axis_index("stn") * own
    basis = basis_table(total_ch)
    mine = lax.dynamic_slice_in_dim(basis, lax.axis_index("chan"), 1, 0)[0]

    msg_rows = rows + COMPS + 8
    msg = pl.pallas_call(
        partial(combine_kernel, paths=paths, comps=sources),
        out_shape=jax.ShapeDtypeStruct((msg_rows, width), f32),
        in_specs=[SM, VM, VM, VM],
        out_specs=VM,
        compiler_params=params(),
        name="combine",
    )(pointing[:, 0], model.reshape(COMPS * sources, width), vis[0], pairs)

    own_at = lax.axis_index("stn")
    whole = jnp.zeros((msg_rows, total_base), f32)
    whole = lax.dynamic_update_slice(whole, msg, (0, own_at * width))
    for d in range(1, blocks):
        got = lax.ppermute(msg, "stn", [(i, (i + d) % blocks) for i in range(blocks)])
        whole = lax.dynamic_update_slice(whole, got, (0, (own_at - d) % blocks * width))

    def shape(*dims, dtype=f32):
        return jax.ShapeDtypeStruct(dims, dtype)

    state = [shape(rows, total_base)] * 3 + [shape(8, total_base), shape(8, LANES)]
    gather_scratch = [pltpu.VMEM((rows, width), f32)] * 2
    sum_scratch = [pltpu.VMEM((24 * paths, width), bf16)] * 2 + [pltpu.VMEM((12 * paths, stations), f32)]

    gain_now = gains.reshape(rows, stations)
    dual_now = dual.reshape(rows, stations)
    ohp, ohq, x, y, h, e, energy = pl.pallas_call(
        partial(first_kernel, plan=plan),
        out_shape=[shape(plan.window, total_base, dtype=bf16), shape(stations, total_base, dtype=bf16)] + state,
        in_specs=[VM, VM],
        out_specs=[VM] * 7,
        scratch_shapes=gather_scratch,
        compiler_params=params(40 << 20),
        name="first",
    )(gain_now, whole)

    def exchange(array):
        return lax.all_to_all(jnp.broadcast_to(array[None], (chans,) + array.shape), "chan", 0, 0)

    poly_now = poly.reshape(TERMS, rows, stations)
    consensus = sum(mine[t] * poly_now[t] for t in range(TERMS))
    anchor = consensus - dual_now
    steps = STEPS * INNER
    for n in range(steps):
        got = exchange(energy).reshape(chans * 8, LANES)[::8]
        if n < steps - 1:
            gain_now, x, y, h, e, energy = pl.pallas_call(
                partial(middle_kernel, plan=plan, count=count),
                out_shape=[shape(rows, stations)] + state,
                in_specs=[SM] + [VM] * 10,
                out_specs=[VM] * 6,
                scratch_shapes=gather_scratch + sum_scratch,
                compiler_params=params(40 << 20),
                name="middle",
            )(rhos, gain_now, anchor, got, whole, ohp, ohq, x, y, h, e)
        else:
            gain_now = pl.pallas_call(
                partial(last_kernel, plan=plan, count=count),
                out_shape=shape(rows, stations),
                in_specs=[SM] + [VM] * 9,
                out_specs=VM,
                scratch_shapes=sum_scratch,
                compiler_params=params(40 << 20),
                name="last",
            )(rhos, gain_now, anchor, got, ohp, ohq, x, y, h, e)
        if n % INNER == INNER - 1:
            tilted = gain_now + dual_now
            if n == steps - 1:
                tilted = lax.dynamic_slice(tilted, (0, block_start), (rows, own))
                gain_own = lax.dynamic_slice(gain_now, (0, block_start), (rows, own))
            all_ch = exchange(tilted)
            fit = [
                sum(basis[f, t] * all_ch[f] for f in range(total_ch)) / total_ch
                for t in range(TERMS)
            ]
            consensus = sum(mine[t] * fit[t] for t in range(TERMS))
            dual_now = tilted - consensus
            anchor = consensus - dual_now
    out = (1, COMPS, paths, own)
    return (
        gain_own.reshape(out),
        dual_now.reshape(out),
        jnp.stack(fit, axis=0).reshape((TERMS,) + out[1:]),
    )


def solution(mesh):
    placed = (
        P("chan", None, "stn"),
        P("chan", None, None, "stn"),
        P(),
        P(None, "stn"),
        P("chan", None, None, None),
        P(),
        P("chan", None, None, None),
        P(),
    )
    return jax.shard_map(
        partial(body, chans=mesh.shape["chan"], blocks=mesh.shape["stn"]),
        mesh=mesh,
        in_specs=placed,
        out_specs=(
            P("chan", None, None, "stn"),
            P("chan", None, None, "stn"),
            P(None, None, None, "stn"),
        ),
        check_vma=False,
    )
```

time: 538 us -> 208 us (0.39)
  waiting for transfers between devices: 192 us -> 41.3 us
  blocking collectives: 163 us -> 16.5 us
  local copies, waits for them, and re-layouts: 111 us -> 53.4 us
  Pallas kernels: 0 us -> 33.7 us
  starting transfers between devices: 0.47 us -> 21.8 us
  matrix products: 17.9 us -> 0 us
  between operations: 21.2 us -> 6.17 us
    psum x6 -> x0, waiting for transfers between devices: 192 us -> none  [the longest x4 132 us: body(): whole_accumulated_totals = lax.psum(least_squares_equations, 'stn')]
    psum x4 -> x0, blocking collectives: 163 us -> none  [body(): lax.psum(jnp.sum(chan_state[5]), ('chan', 'stn')) / sample_count]
    gather x16 -> x0, local copies, waits for them, and re-layouts: 95.1 us -> none  [the longest x8 47.6 us: channel_state(): second_gain = entries(spectral_jones_matrices[:, :, antenna_pairs[1]])]
    unnamed x37 -> x94, local copies, waits for them, and re-layouts: 5.05 us -> 46.6 us
    pallas_call x0 -> x6, Pallas kernels: none -> 33.7 us  [the longest x3 23.7 us: body(): pl.pallas_call(partial(middle_kernel, plan=plan, count=count), out_shape=...]
    all_to_all x0 -> x4, waiting for transfers between devices: none -> 21.7 us  [exchange(): lax.all_to_all(jnp.broadcast_to(array[None], (chans,) + array.shape), 'ch...]
    ppermute x0 -> x3, waiting for transfers between devices: none -> 19.6 us  [body(): lax.ppermute(msg, 'stn', [(i, (i + d) % blocks) for i in range(blocks)])]
    dot_general x12 -> x0, matrix products: 17.9 us -> none  [the longest x4 9.3 us: channel_sums(): jnp.einsum('pkb,bs->pks', first_parts, first_table, precision=highest)]
  transfers between devices with their start and end apart: 6 -> 7, of which waited for: 6 -> 6; matrix products, arithmetic and copies ran while one was open for 2% -> 5% of each run, Pallas kernels for 0% -> 0%
where the time goes in v1:
time: 208 us; the launch traced here: 206 us
  local copies, waits for them, and re-layouts  53.4 us (26%)
  waiting for transfers between devices  41.3 us (20%)
  Pallas kernels  33.7 us (16%)
  other arithmetic  32.7 us (16%)
  starting transfers between devices  21.8 us (10%)
  blocking collectives  16.5 us (8%)
  between operations  6.17 us (3%)
    unnamed x94, local copies, waits for them, and re-layouts  46.6 us
    pallas_call x3, Pallas kernels, body(): pl.pallas_call(partial(middle_kernel, plan=plan, count=count), out_shape=...  23.7 us
    all_to_all x4, waiting for transfers between devices, exchange(): lax.all_to_all(jnp.broadcast_to(array[None], (chans,) + array.shape), 'ch...  21.7 us
    ppermute x3, waiting for transfers between devices, body(): lax.ppermute(msg, 'stn', [(i, (i + d) % blocks) for i in range(blocks)])  19.6 us
    all_to_all x2, blocking collectives, exchange(): lax.all_to_all(jnp.broadcast_to(array[None], (chans,) + array.shape), 'ch...  16.5 us
    all_to_all x4, starting transfers between devices, exchange(): lax.all_to_all(jnp.broadcast_to(array[None], (chans,) + array.shape), 'ch...  15.7 us
    sub x1, other arithmetic, body(): dual_now = tilted - consensus  12.1 us
    another operation x4, other arithmetic, body(): jnp.stack(fit, axis=0).reshape((TERMS,) + out[1:])  10.6 us
  transfers between devices with their start and end apart: 7, of which 6 were waited for; matrix products, arithmetic and copies ran while one was open for 5% of the time, Pallas kernels for 0%

profile of v1, /device:TPU:0, one launch (start us, length us, event | category | flops | bytes accessed | tf_op | source)
XLA Modules:
  0.0 205.6 jit_solution(15431641914522852509)
XLA Ops:
  0.6 1.0 copy-done.29
  3.8 1.0 combine.1
  4.8 5.1 %collective-permute-start.2 = (f32[80,1024]{1,0:T(8,128)S(1)}, f32[80,1024]{1,0:T(8,128)S(1)}, u32[]{:S(2)}, u32[]{:S(2)}) collective-permute-start(f32[80,1024]{1,0:T(8,128)S(1)} %combine.1), channel_id=1, source_target_pairs={{0,3},{1,0},{2,1},{3,2},{4,7},{5,4},{6,5},{7,6},{8,11},{9,8},{10,9... | collective-permute-start | bytes 983048 | tf_op jit(solution)/shard_map/ppermute | solution.py:295
  9.9 1.0 collective-permute-start
  18.2 13.7 %collective-permute-done = f32[80,1024]{1,0:T(8,128)S(1)} collective-permute-done((f32[80,1024]{1,0:T(8,128)S(1)}, f32[80,1024]{1,0:T(8,128)S(1)}, u32[]{:S(2)}, u32[]{:S(2)}) %collective-permute-start) | collective-permute-done | bytes 327712 | tf_op jit(solution)/shard_map/ppermute | solution.py:295
  32.0 5.9 %collective-permute-done.1 = f32[80,1024]{1,0:T(8,128)S(1)} collective-permute-done((f32[80,1024]{1,0:T(8,128)S(1)}, f32[80,1024]{1,0:T(8,128)S(1)}, u32[]{:S(2)}, u32[]{:S(2)}) %collective-permute-start.1) | collective-permute-done | bytes 327712 | tf_op jit(solution)/shard_map/ppermute | solution.py:295
  37.9 4.0 %first.1 = (bf16[128,4096]{1,0:T(8,128)(2,1)S(1)}, bf16[512,4096]{1,0:T(8,128)(2,1)S(1)}, f32[64,4096]{1,0:T(8,128)S(1)}, f32[64,4096]{1,0:T(8,128)S(1)}, f32[64...) custom-call(f32[64,512]{1,0:T(8,128)S(1)} %bitcast.51, ...), custom_call_target="tpu_custom_call" | custom-call | tf_op jit(solution)/shard_map/first/pallas_call | solution.py:307
  41.9 2.0 copy-done
  43.9 1.0 copy-done.9
  44.9 1.0 copy-done.11
  47.2 4.0 %all-to-all-start = ((f32[8,8,128]{2,1,0:T(8,128)}), f32[8,8,128]{2,1,0:T(8,128)}, u32[]{:S(2)}, u32[]{:S(2)}) async-start(f32[8,8,128]{2,1,0:T(8,128)} %broadcast_in_dim.15), calls=%async_computation | async-start | bytes 65536 | tf_op jit(solution)/shard_map/all_to_all | solution.py:318
  51.1 3.0 %bitcast_subtract_fusion.2.anchor_ref = f32[64,512]{1,0:T(8,128)S(1)} fusion(f32[1,8,8,512]{3,2,1,0:T(8,128)} %param.14, f32[3,8,8,512]{3,2,1,0:T(8,128)} %param.13, f32[]{:T(128)} %bitcast.3, f32[]{:T(128)} %bitcast.2, f32[]{:T(128)} %bitcast.1), kind=kLoop, calls=%fused_computation.3 | loop fusion | flops 196608 | bytes 655372 | tf_op jit(solution)/shard_map/sub | solution.py:322
  54.1 1.8 all-to-all-done
  56.8 2.2 %copy-done.1 = bf16[512,4096]{1,0:T(8,128)(2,1)S(1)} copy-done((bf16[512,4096]{1,0:T(8,128)(2,1)S(1)}, bf16[512,4096]{1,0:T(8,128)(2,1)}, u32[]{:S(2)}) %copy-start.1) | copy-done | bytes 4194328
  58.9 1.2 copy-done.10
  60.2 1.2 copy-done.12
  63.2 7.9 %middle.3 = (f32[64,512]{1,0:T(8,128)S(1)}, f32[64,4096]{1,0:T(8,128)S(1)}, f32[64,4096]{1,0:T(8,128)S(1)}, f32[64,4096]{1,0:T(8,128)S(1)}, f32[8,4096]{1,0:T(8,128)S(1)}, /*index=5*/f32[8,128]{1,0:T(8,128)S(1)}) custom-call(f32[8]{0:T(128)S(1)} %copy-done.44, f32[64,512]{1,0:T(8,128)S(1)} %bitcast.52, f32[64,512]{1,0:T(8,128)S(1)} %bitcast_subtract_fusion.2.anchor_ref, ...), custom_call_target="tpu_custom_call" | custom-call | tf_op jit(solution)/shard_map/middle/pallas_call | solution.py:327
  72.1 1.0 copy-done.15
  73.1 1.0 copy-done.17
  75.4 7.2 %all_to_all.30 = f32[8,8,128]{2,1,0:T(8,128)S(1)} all-to-all(f32[8,8,128]{2,1,0:T(8,128)S(1)} %broadcast_in_dim.16), channel_id=1, replica_groups=mesh['chan'=8,'stn'=4] {'chan'}, dimensions={0} | all-to-all | bytes 65536 | tf_op jit(solution)/shard_map/all_to_all | solution.py:318
  82.6 2.2 %copy-done.2 = bf16[512,4096]{1,0:T(8,128)(2,1)S(1)} copy-done((bf16[512,4096]{1,0:T(8,128)(2,1)S(1)}, bf16[512,4096]{1,0:T(8,128)(2,1)}, u32[]{:S(2)}) %copy-start.2) | copy-done | bytes 4194328
  84.8 1.2 copy-done.14
  86.0 1.2 copy-done.16
  87.3 1.2 copy-done.18
  90.3 7.9 %middle.4 = (f32[64,512]{1,0:T(8,128)S(1)}, f32[64,4096]{1,0:T(8,128)S(1)}, f32[64,4096]{1,0:T(8,128)S(1)}, f32[64,4096]{1,0:T(8,128)S(1)}, f32[8,4096]{1,0:T(8,128)S(1)}, /*index=5*/f32[8,128]{1,0:T(8,128)S(1)}) custom-call(f32[8]{0:T(128)S(1)} %copy-done.44, f32[64,512]{1,0:T(8,128)S(1)} %copy-done.39, f32[64,512]{1,0:T(8,128)S(1)} %bitcast_subtract_fusion.2.anchor_ref, ...), custom_call_target="tpu_custom_call" | custom-call | tf_op jit(solution)/shard_map/middle/pallas_call | solution.py:327
  99.2 1.0 copy-done.7
  102.1 4.0 %all-to-all-start.3 = ((f32[8,8,128]{2,1,0:T(8,128)}), f32[8,8,128]{2,1,0:T(8,128)}, u32[]{:S(2)}, u32[]{:S(2)}) async-start(f32[8,8,128]{2,1,0:T(8,128)} %broadcast_in_dim.18), calls=%async_computation.3 | async-start | bytes 65536 | tf_op jit(solution)/shard_map/all_to_all | solution.py:318
  106.1 1.0 bitcast_add_fusion
  107.1 3.9 %all-to-all-done.3 = f32[8,8,128]{2,1,0:T(8,128)} async-done(((f32[8,8,128]{2,1,0:T(8,128)}), f32[8,8,128]{2,1,0:T(8,128)}, u32[]{:S(2)}, u32[]{:S(2)}) %all-to-all-start.3) | async-done | bytes 32800 | tf_op jit(solution)/shard_map/all_to_all | solution.py:318
  110.9 1.2 broadcast_in_dim.17
  112.1 4.4 %all-to-all-start.2 = ((f32[8,64,512]{2,1,0:T(8,128)}), f32[8,64,512]{2,1,0:T(8,128)}, u32[]{:S(2)}, u32[]{:S(2)}) async-start(f32[8,64,512]{2,1,0:T(8,128)} %broadcast_in_dim.17), calls=%async_computation.2 | async-start | bytes 2097152 | tf_op jit(solution)/shard_map/all_to_all | solution.py:318
  120.6 11.2 %all-to-all-done.2 = f32[8,64,512]{2,1,0:T(8,128)} async-done(((f32[8,64,512]{2,1,0:T(8,128)}), f32[8,64,512]{2,1,0:T(8,128)}, u32[]{:S(2)}, u32[]{:S(2)}) %all-to-all-start.2) | async-done | bytes 1048608 | tf_op jit(solution)/shard_map/all_to_all | solution.py:318
  131.8 12.1 %bitcast_subtract_fusion.1 = (f32[64,512]{1,0:T(8,128)}, f32[1,64,512]{2,1,0:T(8,128)S(1)}) fusion(f32[64,512]{1,0:T(8,128)S(1)} %bitcast_add_fusion, f32[]{:T(128)S(6)} %mul.495, f32[]{:T(128)} %bitcast.26, f32[]{:T(128)} %bitcast.25, f32[]{:T(128)} %bitcast.24, f32[]{:T(128)} %bitcast.23, f32[]{:T(128)} %bitcast.22, f32[]{:T(128)} %bitcast.21, f32[]{:T(128)} %bitcast.20, ...), kind=kLoop, calls=%fused_computation.1 | loop fusion | flops 1409024 | bytes 1441868 | tf_op jit(solution)/shard_map/sub | solution.py:357
  144.8 2.2 %copy-done.3 = bf16[512,4096]{1,0:T(8,128)(2,1)S(1)} copy-done((bf16[512,4096]{1,0:T(8,128)(2,1)S(1)}, bf16[512,4096]{1,0:T(8,128)(2,1)}, u32[]{:S(2)}) %copy-start.3) | copy-done | bytes 4194328
  147.0 1.2 copy-done.8
  150.0 7.9 %middle.5 = (f32[64,512]{1,0:T(8,128)S(1)}, f32[64,4096]{1,0:T(8,128)S(1)}, f32[64,4096]{1,0:T(8,128)S(1)}, f32[64,4096]{1,0:T(8,128)S(1)}, f32[8,4096]{1,0:T(8,128)S(1)}, /*index=5*/f32[8,128]{1,0:T(8,128)S(1)}) custom-call(f32[8]{0:T(128)S(1)} %copy-done.44, f32[64,512]{1,0:T(8,128)S(1)} %copy-done.26, f32[64,512]{1,0:T(8,128)S(1)} %bitcast_subtract_fusion.anchor_ref, ...), custom_call_target="tpu_custom_call" | custom-call | tf_op jit(solution)/shard_map/middle/pallas_call | solution.py:327
  159.9 1.0 copy-done.23
  162.8 3.3 %all-to-all-start.4 = ((f32[8,8,128]{2,1,0:T(8,128)}), f32[8,8,128]{2,1,0:T(8,128)S(1)}, u32[]{:S(2)}, u32[]{:S(2)}) async-start(f32[8,8,128]{2,1,0:T(8,128)} %broadcast_in_dim.19), calls=%async_computation.4 | async-start | bytes 65536 | tf_op jit(solution)/shard_map/all_to_all | solution.py:318
  166.2 4.8 %all-to-all-done.4 = f32[8,8,128]{2,1,0:T(8,128)S(1)} async-done(((f32[8,8,128]{2,1,0:T(8,128)}), f32[8,8,128]{2,1,0:T(8,128)S(1)}, u32[]{:S(2)}, u32[]{:S(2)}) %all-to-all-start.4) | async-done | bytes 32800 | tf_op jit(solution)/shard_map/all_to_all | solution.py:318
  171.0 2.2 %copy-done.4 = bf16[512,4096]{1,0:T(8,128)(2,1)S(1)} copy-done((bf16[512,4096]{1,0:T(8,128)(2,1)S(1)}, bf16[512,4096]{1,0:T(8,128)(2,1)}, u32[]{:S(2)}) %copy-start.4) | copy-done | bytes 4194328
  173.1 1.2 copy-done.20
  174.4 1.2 copy-done.22
  175.6 1.2 copy-done.24
  178.6 5.0 %last.1 = f32[64,512]{1,0:T(8,128)S(1)} custom-call(f32[8]{0:T(128)S(1)} %copy-done.44, f32[64,512]{1,0:T(8,128)S(1)} %copy-done.33, f32[64,512]{1,0:T(8,128)S(1)} %bitcast_subtract_fusion.anchor_ref, f32[8,128]{1,0:T(8,128)S(1)} %slice.251.energy_ref, bf16[128,4096]{1,0:T(8,128)(2,1)S(1)} %get-tuple-element.29.ohp_ref, bf16[512,4096]{1,0:T(8,128)(2,1)S(1)} %copy-done.4, ...), custom_call_target="tpu_custom_call" | custom-call | tf_op jit(solution)/shard_map/last/pallas_call | solution.py:337
  183.7 1.4 dynamic-slice_add_fusion
  185.1 9.3 %all_to_all.31 = f32[8,64,128]{2,1,0:T(8,128)S(1)} all-to-all(f32[8,64,128]{2,1,0:T(8,128)S(1)} %broadcast_in_dim.20), channel_id=1, replica_groups=mesh['chan'=8,'stn'=4] {'chan'}, dimensions={0} | all-to-all | bytes 524288 | tf_op jit(solution)/shard_map/all_to_all | solution.py:318
  194.4 5.0 %multiply_bitcast_fusion = (f32[1,8,8,128]{3,2,1,0:T(8,128)S(1)}, f32[1,64,128]{2,1,0:T(8,128)S(1)}) fusion(f32[8,64,128]{2,1,0:T(8,128)S(1)} %all_to_all.31, f32[]{:T(128)} %bitcast.26, f32[]{:T(128)} %bitcast.25, f32[]{:T(128)} %bitcast.24, f32[]{:T(128)} %bitcast.23, f32[]{:T(128)} %bitcast.22, f32[]{:T(128)} %bitcast.21, f32[]{:T(128)} %bitcast.20, ...), kind=kLoop, calls=%fused_computation.12 | loop fusion | flops 131072 | bytes 327712 | tf_op jit(solution)/shard_map/stack | solution.py:363
  199.4 4.9 %multiply_bitcast_fusion.1 = (f32[1,8,8,128]{3,2,1,0:T(8,128)S(1)}, f32[1,64,128]{2,1,0:T(8,128)S(1)}) fusion(f32[8,64,128]{2,1,0:T(8,128)S(1)} %all_to_all.31, f32[]{:T(128)} %bitcast.18, f32[]{:T(128)} %bitcast.17, f32[]{:T(128)} %bitcast.16, f32[]{:T(128)} %bitcast.15, f32[]{:T(128)} %bitcast.14, f32[]{:T(128)} %bitcast.13, f32[]{:T(128)} %bitcast.12, ...), kind=kLoop, calls=%fused_computation.13 | loop fusion | flops 131072 | bytes 327712 | tf_op jit(solution)/shard_map/stack | solution.py:363
  (106 shorter events, 29.0 us)
Async XLA Ops:
  0.6 1.0 copy-start.29
  1.7 0.8 copy-start.42
  2.4 0.7 copy-start.43
  4.8 33.1 %collective-permute-start.2 = (f32[80,1024]{1,0:T(8,128)S(1)}, f32[80,1024]{1,0:T(8,128)S(1)}, u32[]{:S(2)}, u32[]{:S(2)}) collective-permute-start(f32[80,1024]{1,0:T(8,128)S(1)} %combine.1), channel_id=1, source_target_pairs={{0,3},{1,0},{2,1},{3,2},{4,7},{5,4},{6,5},{7,6},{8,11},{9,8},{10,9... | collective-permute-start | bytes 983048 | tf_op jit(solution)/shard_map/ppermute | solution.py:295
  9.9 27.9 %collective-permute-start.1 = (f32[80,1024]{1,0:T(8,128)S(1)}, f32[80,1024]{1,0:T(8,128)S(1)}, u32[]{:S(2)}, u32[]{:S(2)}) collective-permute-start(f32[80,1024]{1,0:T(8,128)S(1)} %combine.1), channel_id=1, source_target_pairs={{0,2},{1,3},{2,0},{3,1},{4,6},{5,7},{6,4},{7,5},{8,10},{9,11},{10,... | collective-permute-start | bytes 983048 | tf_op jit(solution)/shard_map/ppermute | solution.py:295
  9.9 22.0 %collective-permute-start = (f32[80,1024]{1,0:T(8,128)S(1)}, f32[80,1024]{1,0:T(8,128)S(1)}, u32[]{:S(2)}, u32[]{:S(2)}) collective-permute-start(f32[80,1024]{1,0:T(8,128)S(1)} %combine.1), channel_id=1, source_target_pairs={{0,1},{1,2},{2,3},{3,0},{4,5},{5,6},{6,7},{7,4},{8,9},{9,10},{10,1... | collective-permute-start | bytes 983048 | tf_op jit(solution)/shard_map/ppermute | solution.py:295
  17.5 20.5 %copy-start.27 = (f32[1,8,8,512]{3,2,1,0:T(8,128)S(1)}, f32[1,8,8,512]{3,2,1,0:T(8,128)}, u32[]{:S(2)}) copy-start(f32[1,8,8,512]{3,2,1,0:T(8,128)} %param.12) | copy-start | bytes 393220
  37.9 18.9 %copy-start.44 = (f32[8]{0:T(128)S(1)}, f32[8]{0:T(128)}, u32[]{:S(2)}) copy-start(f32[8]{0:T(128)} %rho_ref.7) | copy-start | bytes 100
  41.9 2.0 copy-start
  43.9 1.0 copy-start.9
  44.9 1.0 copy-start.11
  47.2 8.8 %all-to-all-start = ((f32[8,8,128]{2,1,0:T(8,128)}), f32[8,8,128]{2,1,0:T(8,128)}, u32[]{:S(2)}, u32[]{:S(2)}) async-start(f32[8,8,128]{2,1,0:T(8,128)} %broadcast_in_dim.15), calls=%async_computation | async-start | bytes 65536 | tf_op jit(solution)/shard_map/all_to_all | solution.py:318
  56.8 2.2 %copy-start.1 = (bf16[512,4096]{1,0:T(8,128)(2,1)S(1)}, bf16[512,4096]{1,0:T(8,128)(2,1)}, u32[]{:S(2)}) copy-start(bf16[512,4096]{1,0:T(8,128)(2,1)} %copy-done) | copy-start | bytes 12582916
  58.9 1.2 copy-start.10
  60.2 1.2 copy-start.12
  61.4 0.9 copy-start.28
  62.3 0.9 copy-start.37
  71.1 1.0 copy-start.13
  72.1 1.0 copy-start.15
  73.1 1.0 copy-start.17
  74.1 0.7 copy-start.38
  82.6 2.2 %copy-start.2 = (bf16[512,4096]{1,0:T(8,128)(2,1)S(1)}, bf16[512,4096]{1,0:T(8,128)(2,1)}, u32[]{:S(2)}) copy-start(bf16[512,4096]{1,0:T(8,128)(2,1)} %copy-done) | copy-start | bytes 12582916
  84.8 1.2 copy-start.14
  86.0 1.2 copy-start.16
  87.3 1.2 copy-start.18
  88.5 0.9 copy-start.39
  89.4 0.9 copy-start.41
  98.2 1.0 copy-start.5
  99.2 1.0 copy-start.7
  100.8 0.7 copy-start.30
  102.1 8.8 %all-to-all-start.3 = ((f32[8,8,128]{2,1,0:T(8,128)}), f32[8,8,128]{2,1,0:T(8,128)}, u32[]{:S(2)}, u32[]{:S(2)}) async-start(f32[8,8,128]{2,1,0:T(8,128)} %broadcast_in_dim.18), calls=%async_computation.3 | async-start | bytes 65536 | tf_op jit(solution)/shard_map/all_to_all | solution.py:318
  107.1 24.7 %copy-start.46 = (f32[64,512]{1,0:T(8,128)}, f32[64,512]{1,0:T(8,128)S(1)}, u32[]{:S(2)}) copy-start(f32[64,512]{1,0:T(8,128)S(1)} %bitcast_add_fusion) | copy-start | bytes 393220
  112.1 19.7 %all-to-all-start.2 = ((f32[8,64,512]{2,1,0:T(8,128)}), f32[8,64,512]{2,1,0:T(8,128)}, u32[]{:S(2)}, u32[]{:S(2)}) async-start(f32[8,64,512]{2,1,0:T(8,128)} %broadcast_in_dim.17), calls=%async_computation.2 | async-start | bytes 2097152 | tf_op jit(solution)/shard_map/all_to_all | solution.py:318
  131.8 13.0 %copy-start.6 = (f32[64,4096]{1,0:T(8,128)S(1)}, f32[64,4096]{1,0:T(8,128)}, u32[]{:S(2)}) copy-start(f32[64,4096]{1,0:T(8,128)} %copy-done.5) | copy-start | bytes 3145732
  144.8 2.2 %copy-start.3 = (bf16[512,4096]{1,0:T(8,128)(2,1)S(1)}, bf16[512,4096]{1,0:T(8,128)(2,1)}, u32[]{:S(2)}) copy-start(bf16[512,4096]{1,0:T(8,128)(2,1)} %copy-done) | copy-start | bytes 12582916
  147.0 1.2 copy-start.8
  148.2 0.9 copy-start.26
  149.1 0.9 copy-start.31
  157.9 1.0 copy-start.19
  158.9 1.0 copy-start.21
  159.9 1.0 copy-start.23
  162.8 8.1 %all-to-all-start.4 = ((f32[8,8,128]{2,1,0:T(8,128)}), f32[8,8,128]{2,1,0:T(8,128)S(1)}, u32[]{:S(2)}, u32[]{:S(2)}) async-start(f32[8,8,128]{2,1,0:T(8,128)} %broadcast_in_dim.19), calls=%async_computation.4 | async-start | bytes 65536 | tf_op jit(solution)/shard_map/all_to_all | solution.py:318
  171.0 2.2 %copy-start.4 = (bf16[512,4096]{1,0:T(8,128)(2,1)S(1)}, bf16[512,4096]{1,0:T(8,128)(2,1)}, u32[]{:S(2)}) copy-start(bf16[512,4096]{1,0:T(8,128)(2,1)} %copy-done) | copy-start | bytes 12582916
  173.1 1.2 copy-start.20
  174.4 1.2 copy-start.22
  175.6 1.2 copy-start.24
  176.8 0.9 copy-start.33
  177.7 0.9 copy-start.35
  (6 other events, 4.0 us)

commit v2 on v1

v2 whole, which is shorter than its diff:
```python
from functools import partial

import jax
import jax.numpy as jnp
import numpy as np
from jax import lax
from jax.experimental import pallas as pl
from jax.experimental.pallas import tpu as pltpu
from jax.sharding import PartitionSpec as P

TERMS = 3
STEPS = 2
INNER = 2
COMPS = 8
LANES = 128

student_nu = 2.0
squared_tolerance = 1e-06
f32 = jnp.float32
bf16 = jnp.bfloat16


def cmul(a, b):
    return (a[0] * b[0] - a[1] * b[1], a[0] * b[1] + a[1] * b[0])


def cadd(a, b):
    return (a[0] + b[0], a[1] + b[1])


def conj(a):
    return (a[0], -a[1])


def mmul(a, b):
    return [
        cadd(cmul(a[0], b[0]), cmul(a[1], b[2])),
        cadd(cmul(a[0], b[1]), cmul(a[1], b[3])),
        cadd(cmul(a[2], b[0]), cmul(a[3], b[2])),
        cadd(cmul(a[2], b[1]), cmul(a[3], b[3])),
    ]


def adj(m):
    return [conj(m[0]), conj(m[2]), conj(m[1]), conj(m[3])]


def flat(m):
    return [m[i][0] for i in range(4)] + [m[i][1] for i in range(4)]


def square(a):
    return a[0] * a[0] + a[1] * a[1]


def gram(m):
    cross = cadd(cmul(m[0], conj(m[2])), cmul(m[1], conj(m[3])))
    return [
        square(m[0]) + square(m[1]),
        square(m[2]) + square(m[3]),
        cross[0],
        cross[1],
    ]


def basis_table(channel_count):
    frequency = (2.0 * np.arange(channel_count) + 1.0) / channel_count - 1.0
    columns = []
    for degree in range(TERMS):
        column = frequency**degree
        for earlier in columns:
            column = column - np.sum(earlier * column) / channel_count * earlier
        columns.append(column / np.sqrt(np.sum(column * column) / channel_count))
    return np.stack(columns, axis=1).astype(np.float32)


def split(x):
    hi = x.astype(bf16)
    lo = (x - hi.astype(f32)).astype(bf16)
    return hi, lo


def load(ref, paths, lanes):
    rows = [ref[c * paths : (c + 1) * paths, lanes] for c in range(COMPS)]
    return [(rows[i], rows[4 + i]) for i in range(4)]


class Plan:
    def __init__(self, paths, stations, blocks, chans, width):
        self.paths, self.stations = paths, stations
        self.blocks, self.width, self.chans = blocks, width, chans
        self.rows = COMPS * paths
        self.own = stations // blocks
        self.window = min(stations, max(self.own, LANES))
        self.centre = max(blocks // 2 - 1, 0)
        self.order = [i for i in range(blocks) if i != self.centre]

    def mirror(self, i):
        return self.blocks - 1 - i

    def inward(self):
        low, high = self.centre, self.mirror(self.centre)
        if low == high:
            return []
        return [[(i, low), (self.mirror(i), high)] for i in self.order]

    def outward(self):
        low, high = self.centre, self.mirror(self.centre)
        return [[(low, low - i), (high, high + i)] for i in range(1, self.centre + 1)]

    def slots(self):
        low = [[z] + self.order for z in range((self.blocks + 1) // 2)]
        high = [[z] + [self.mirror(i) for i in self.order] for z in range((self.blocks + 1) // 2, self.blocks)]
        return np.asarray(low + high, np.int32)


def radices(count):
    out = []
    while count > 1:
        step = 2 if not out and (count.bit_length() - 1) % 2 else 4
        out.append(step)
        count //= step
    return out


def partners(count, distance):
    return [(i, i ^ distance) for i in range(count)]


def chan_sum(x, count):
    span = 1
    for radix in radices(count):
        got = [lax.ppermute(x, "chan", partners(count, d * span)) for d in range(1, radix)]
        for y in got:
            x = x + y
        span *= radix
    return x


def chan_gather(x, count):
    x = x[None]
    span = 1
    for radix in radices(count):
        got = [lax.ppermute(x, "chan", partners(count, d * span)) for d in range(1, radix)]
        x = jnp.concatenate([x] + got, axis=0)
        span *= radix
    return x


def combine_kernel(point_ref, model_hbm, vis_hbm, pair_hbm, out_ref, model_ref, vis_ref, pair_ref,
                   sems, *, paths, comps):
    copies = [
        pltpu.make_async_copy(model_hbm, model_ref, sems.at[0]),
        pltpu.make_async_copy(vis_hbm, vis_ref, sems.at[1]),
        pltpu.make_async_copy(pair_hbm, pair_ref, sems.at[2]),
    ]
    for copy in copies:
        copy.start()
    for copy in copies:
        copy.wait()
    width = out_ref.shape[1]
    which = lax.broadcasted_iota(jnp.int32, (paths, width), 0)
    for c in range(COMPS):
        total = jnp.zeros((paths, width), f32)
        for s in range(comps):
            row = model_ref[c * comps + s : c * comps + s + 1, :]
            total = total + jnp.where(which == point_ref[s], row, 0.0)
        out_ref[c * paths : (c + 1) * paths, :] = total
    base = COMPS * paths
    out_ref[base : base + COMPS, :] = vis_ref[...]
    out_ref[base + COMPS : base + COMPS + 2, :] = pair_ref[...].astype(f32)
    out_ref[base + COMPS + 2 :, :] = jnp.zeros((6, width), f32)


def window_of(plan, starts_ref, slot):
    return pl.ds(pl.multiple_of(starts_ref[slot], LANES if plan.window % LANES == 0 else plan.window), plan.window)


def make_onehots(plan, starts_ref, msg_refs, ohp_ref, ohq_ref):
    width, base = plan.width, plan.rows + COMPS
    for i, msg_ref in enumerate(msg_refs):
        lanes = slice(i * width, (i + 1) * width)
        first = msg_ref[base : base + 1, :].astype(jnp.int32) - starts_ref[i]
        second = msg_ref[base + 1 : base + 2, :].astype(jnp.int32)
        pos = lax.broadcasted_iota(jnp.int32, (plan.window, width), 0)
        ohp_ref[:, lanes] = jnp.where(pos == first, 1.0, 0.0).astype(bf16)
        pos = lax.broadcasted_iota(jnp.int32, (plan.stations, width), 0)
        ohq_ref[:, lanes] = jnp.where(pos == second, 1.0, 0.0).astype(bf16)


def residuals(plan, starts_ref, gains, msg_refs, ohp_ref, ohq_ref, keep, both_ref, jp_ref, jq_ref):
    paths, rows, width = plan.paths, plan.rows, plan.width
    hi, lo = split(gains)
    both_ref[0:rows, :] = hi
    both_ref[rows : 2 * rows, :] = lo
    total = jnp.zeros((1, LANES), f32)
    for i, msg_ref in enumerate(msg_refs):
        block = slice(i * width, (i + 1) * width)
        got = jnp.dot(both_ref[...], ohq_ref[:, block], preferred_element_type=f32)
        jq_ref[...] = got[:rows] + got[rows:]
        near = both_ref[:, window_of(plan, starts_ref, i)]
        got = jnp.dot(near, ohp_ref[:, block], preferred_element_type=f32)
        jp_ref[...] = got[:rows] + got[rows:]

        def piece(t, carry):
            here = pl.ds(pl.multiple_of(t * LANES, LANES), LANES)
            there = pl.ds(pl.multiple_of(i * width + t * LANES, LANES), LANES)
            coherent = load(msg_ref, paths, here)
            y = mmul(coherent, adj(load(jq_ref, paths, here)))
            first = load(jp_ref, paths, here)
            g = flat(mmul(first, y))
            energy = jnp.zeros((1, LANES), f32)
            for c in range(COMPS):
                r = msg_ref[rows + c : rows + c + 1, here] - jnp.sum(g[c], axis=0, keepdims=True)
                energy = energy + r * r
                if keep is not None:
                    keep[0][c * paths : (c + 1) * paths, there] = r + g[c]
            if keep is not None:
                for c, v in enumerate(flat(y)):
                    keep[1][c * paths : (c + 1) * paths, there] = v
                for c, v in enumerate(flat(mmul(first, coherent))):
                    keep[2][c * paths : (c + 1) * paths, there] = v
                keep[3][0:1, there] = energy
            return carry + energy

        total = lax.fori_loop(0, width // LANES, piece, total)
    return total


def normal_sums(plan, starts_ref, noise, ohp_ref, ohq_ref, keep, fp_ref, sp_ref, acc_ref):
    paths, width = plan.paths, plan.width
    half = 12 * paths
    contract = (((1,), (1,)), ((), ()))
    x_ref, y_ref, h_ref, e_ref = keep
    for i in range(plan.blocks):
        block = slice(i * width, (i + 1) * width)

        def piece(t, carry):
            here = pl.ds(pl.multiple_of(t * LANES, LANES), LANES)
            there = pl.ds(pl.multiple_of(i * width + t * LANES, LANES), LANES)
            weight = (student_nu + 2.0) / (student_nu + e_ref[0:1, there] / noise)
            weight = jnp.broadcast_to(weight, (paths, LANES))
            x = [(a * weight, b * weight) for a, b in load(x_ref, paths, there)]
            y = load(y_ref, paths, there)
            parts = [v * weight for v in gram(y)] + flat(mmul(x, adj(y)))
            hi, lo = split(jnp.concatenate(parts, axis=0))
            fp_ref[0:half, here] = hi
            fp_ref[half : 2 * half, here] = lo
            h = load(h_ref, paths, there)
            parts = [v * weight for v in gram(adj(h))] + flat(mmul(adj(x), h))
            hi, lo = split(jnp.concatenate(parts, axis=0))
            sp_ref[0:half, here] = hi
            sp_ref[half : 2 * half, here] = lo
            return carry

        lax.fori_loop(0, width // LANES, piece, 0)
        got = lax.dot_general(sp_ref[...], ohq_ref[:, block], contract, preferred_element_type=f32)
        got = got[:half] + got[half:]
        if i == 0:
            acc_ref[...] = got
        else:
            acc_ref[...] += got
        got = lax.dot_general(fp_ref[...], ohp_ref[:, block], contract, preferred_element_type=f32)
        acc_ref[:, window_of(plan, starts_ref, i)] += got[:half] + got[half:]


def solve(plan, acc_ref, anchor, gains, rho_ref):
    paths = plan.paths
    which = lax.broadcasted_iota(jnp.int32, (paths, plan.stations), 0)
    rho = jnp.zeros((paths, plan.stations), f32)
    for k in range(paths):
        rho = jnp.where(which == k, rho_ref[k], rho)
    part = [acc_ref[c * paths : (c + 1) * paths, :] for c in range(12)]
    a, d = part[0] + rho, part[1] + rho
    inv = 1.0 / (a * d - part[2] * part[2] - part[3] * part[3])
    a, d, c0, c1 = a * inv, d * inv, part[2] * inv, part[3] * inv
    rhs = [part[4 + c] + rho * anchor[c * paths : (c + 1) * paths] for c in range(COMPS)]
    out = [None] * COMPS
    for row in (0, 2):
        u = (rhs[row], rhs[4 + row])
        v = (rhs[row + 1], rhs[5 + row])
        left = cmul(v, (c0, -c1))
        right = cmul(u, (c0, c1))
        out[row], out[4 + row] = u[0] * d - left[0], u[1] * d - left[1]
        out[row + 1], out[5 + row] = v[0] * a - right[0], v[1] * a - right[1]
    return 0.5 * (gains + jnp.concatenate(out, axis=0))


def noise_of(energy, count):
    per_lane = jnp.sum(energy, axis=0, keepdims=True)
    return jnp.sum(per_lane, axis=1, keepdims=True) / count + squared_tolerance


def fit_of(plan, basis_ref, index, fields):
    return [
        sum(basis_ref[lax.bitwise_xor(index, d), t] * field for d, field in enumerate(fields))
        / plan.chans
        for t in range(TERMS)
    ]


def consensus_of(basis_ref, index, fit):
    return sum(basis_ref[index, t] * fit[t] for t in range(TERMS))


def local_kernel(starts_ref, gain_ref, msg_ref, sum_ref, ohp_ref, ohq_ref, both_ref, jp_ref, jq_ref, *, plan):
    make_onehots(plan, starts_ref, [msg_ref], ohp_ref, ohq_ref)
    total = residuals(plan, starts_ref, gain_ref[...], [msg_ref], ohp_ref, ohq_ref, None,
                      both_ref, jp_ref, jq_ref)
    put_sum(sum_ref, total)


def put_sum(sum_ref, total):
    sum_ref[...] = jnp.zeros(sum_ref.shape, f32)
    sum_ref[0:1, :] = total


def first_kernel(rho_ref, starts_ref, basis_ref, index_ref, gain_ref, poly_ref, dual_ref, energy_ref,
                 *refs, plan, count):
    msg_refs, refs = refs[: plan.blocks], refs[plan.blocks :]
    ohp_ref, ohq_ref, gain_out, *refs = refs
    keep, (sum_ref, both_ref, jp_ref, jq_ref, fp_ref, sp_ref, acc_ref) = refs[:4], refs[4:]
    make_onehots(plan, starts_ref, msg_refs, ohp_ref, ohq_ref)
    gather = (msg_refs, ohp_ref, ohq_ref, keep, both_ref, jp_ref, jq_ref)
    residuals(plan, starts_ref, gain_ref[...], *gather)
    noise = noise_of(energy_ref[...], count)
    normal_sums(plan, starts_ref, noise, ohp_ref, ohq_ref, keep, fp_ref, sp_ref, acc_ref)
    anchor = consensus_of(basis_ref, index_ref[0], [poly_ref[t] for t in range(TERMS)]) - dual_ref[...]
    gains = solve(plan, acc_ref, anchor, gain_ref[...], rho_ref)
    gain_out[...] = gains
    put_sum(sum_ref, residuals(plan, starts_ref, gains, *gather))


def turn_kernel(rho_ref, starts_ref, basis_ref, index_ref, gain_ref, poly_ref, dual_ref, energy_ref,
                ohp_ref, ohq_ref, *refs, plan, count):
    keep, (gain_out, tilt_out, fp_ref, sp_ref, acc_ref) = refs[:4], refs[4:]
    noise = noise_of(energy_ref[...], count)
    normal_sums(plan, starts_ref, noise, ohp_ref, ohq_ref, keep, fp_ref, sp_ref, acc_ref)
    anchor = consensus_of(basis_ref, index_ref[0], [poly_ref[t] for t in range(TERMS)]) - dual_ref[...]
    gains = solve(plan, acc_ref, anchor, gain_ref[...], rho_ref)
    gain_out[...] = gains
    tilt_out[...] = gains + dual_ref[...]


def residual_kernel(starts_ref, gain_ref, ohp_ref, ohq_ref, *refs, plan):
    msg_refs, refs = refs[: plan.blocks], refs[plan.blocks :]
    keep, (sum_ref, both_ref, jp_ref, jq_ref) = refs[:4], refs[4:]
    put_sum(sum_ref, residuals(plan, starts_ref, gain_ref[...], msg_refs, ohp_ref, ohq_ref, keep,
                               both_ref, jp_ref, jq_ref))


def normal_kernel(starts_ref, energy_ref, ohp_ref, ohq_ref, *refs, plan, count):
    keep, (acc_ref, fp_ref, sp_ref) = refs[:4], refs[4:]
    noise = noise_of(energy_ref[...], count)
    normal_sums(plan, starts_ref, noise, ohp_ref, ohq_ref, keep, fp_ref, sp_ref, acc_ref)


def resume_kernel(rho_ref, starts_ref, basis_ref, index_ref, gain_ref, field_ref, acc_ref, ohp_ref, ohq_ref,
                  *refs, plan):
    msg_refs, refs = refs[: plan.blocks], refs[plan.blocks :]
    gain_out, dual_out, *refs = refs
    keep, (sum_ref, both_ref, jp_ref, jq_ref) = refs[:4], refs[4:]
    fit = fit_of(plan, basis_ref, index_ref[0], [field_ref[d] for d in range(plan.chans)])
    consensus = consensus_of(basis_ref, index_ref[0], fit)
    dual = field_ref[0] - consensus
    dual_out[...] = dual
    gains = solve(plan, acc_ref, consensus - dual, gain_ref[...], rho_ref)
    gain_out[...] = gains
    put_sum(sum_ref, residuals(plan, starts_ref, gains, msg_refs, ohp_ref, ohq_ref, keep,
                               both_ref, jp_ref, jq_ref))


def last_kernel(rho_ref, starts_ref, basis_ref, index_ref, gain_ref, field_ref, dual_ref, energy_ref,
                ohp_ref, ohq_ref, *refs, plan, count):
    keep, refs = refs[:4], refs[4:]
    outs, (fp_ref, sp_ref, acc_ref) = refs[:-3], refs[-3:]
    noise = noise_of(energy_ref[...], count)
    normal_sums(plan, starts_ref, noise, ohp_ref, ohq_ref, keep, fp_ref, sp_ref, acc_ref)
    fit = fit_of(plan, basis_ref, index_ref[0], [field_ref[d] for d in range(plan.chans)])
    consensus = consensus_of(basis_ref, index_ref[0], fit)
    gains = solve(plan, acc_ref, consensus - dual_ref[...], gain_ref[...], rho_ref)
    tilted = gains + dual_ref[...]
    rows, own = plan.rows, plan.own
    for n, out_ref in enumerate(outs):
        block = index_ref[1] + n * index_ref[2]
        for b in range(plan.blocks):

            @pl.when(block == b)
            def _():
                out_ref[0:rows, :] = gains[:, b * own : (b + 1) * own]
                out_ref[rows : 2 * rows, :] = tilted[:, b * own : (b + 1) * own]


def final_kernel(basis_ref, index_ref, field_ref, fit_out, dual_out, *, plan):
    fit = fit_of(plan, basis_ref, index_ref[0], [field_ref[d] for d in range(plan.chans)])
    for t in range(TERMS):
        fit_out[t] = fit[t]
    dual_out[...] = field_ref[0] - consensus_of(basis_ref, index_ref[0], fit)


VM = pl.BlockSpec(memory_space=pltpu.VMEM)
SM = pl.BlockSpec(memory_space=pltpu.SMEM)
ANY = pl.BlockSpec(memory_space=pl.ANY)


def shape(*dims, dtype=f32):
    return jax.ShapeDtypeStruct(dims, dtype)


def call(kernel, name, smem, arrays, outs, scratch, flops, limit=8 << 20, any_space=False):
    return pl.pallas_call(
        kernel,
        out_shape=outs,
        in_specs=[SM] * len(smem) + [ANY if any_space else VM] * len(arrays),
        out_specs=jax.tree.map(lambda _: VM, outs),
        scratch_shapes=scratch,
        compiler_params=pltpu.CompilerParams(vmem_limit_bytes=limit),
        cost_estimate=pl.CostEstimate(flops=flops, bytes_accessed=1 << 20, transcendentals=0),
        name=name,
    )(*smem, *arrays)


def body(vis, model, pointing, pairs, gains, poly, dual, rhos, *, chans, blocks):
    paths, stations = gains.shape[2], gains.shape[3]
    sources, width = model.shape[2], model.shape[3]
    plan = Plan(paths, stations, blocks, chans, width)
    rows, own = plan.rows, plan.own
    total_base = blocks * width
    count = float(chans * total_base)
    me, z = lax.axis_index("chan"), lax.axis_index("stn")
    basis = jnp.asarray(basis_table(chans))
    slots = jnp.asarray(plan.slots())[z]
    starts = slots * own // plan.window * plan.window
    outward = jnp.where(z <= plan.centre, -1, 1)
    index = jnp.stack([me, z, outward]).astype(jnp.int32)
    tables = (rhos, starts, basis, index)

    msg_rows = rows + COMPS + 8
    msg = call(
        partial(combine_kernel, paths=paths, comps=sources), "combine",
        (pointing[:, 0],), (model.reshape(COMPS * sources, width), vis[0], pairs),
        shape(msg_rows, width),
        [pltpu.VMEM((COMPS * sources, width), f32), pltpu.VMEM((COMPS, width), f32),
         pltpu.VMEM((2, width), jnp.int32), pltpu.SemaphoreType.DMA((3,))],
        1 << 24, any_space=True,
    )
    msgs = [msg] + [lax.ppermute(msg, "stn", pairs_of) for pairs_of in plan.inward()]

    tile = shape(8, LANES)
    keep = [shape(rows, total_base)] * 3 + [shape(8, total_base)]
    gather_scratch = [pltpu.VMEM((2 * rows, stations), bf16)] + [pltpu.VMEM((rows, width), f32)] * 2
    parts_scratch = [pltpu.VMEM((24 * paths, width), bf16)] * 2
    acc_scratch = [pltpu.VMEM((12 * paths, stations), f32)]
    acc_shape = shape(12 * paths, stations)
    field = shape(rows, stations)
    work = 1 << 31

    gain = gains.reshape(rows, stations)
    dual = dual.reshape(rows, stations)
    poly = poly.reshape(TERMS, rows, stations)
    energy = call(
        partial(local_kernel, plan=plan), "local", (starts,), (gain, msg), tile,
        [pltpu.VMEM((plan.window, width), bf16), pltpu.VMEM((stations, width), bf16)] + gather_scratch,
        work // 8,
    )
    energy = chan_sum(energy, chans)
    energy = jnp.concatenate(
        [energy] + [lax.ppermute(energy, "stn", pairs_of) for pairs_of in plan.inward()], axis=0
    )
    ohp, ohq, gain, *state, energy = call(
        partial(first_kernel, plan=plan, count=count), "first", tables,
        (gain, poly, dual, energy, *msgs),
        [shape(plan.window, total_base, dtype=bf16), shape(stations, total_base, dtype=bf16), field]
        + keep + [tile],
        gather_scratch + parts_scratch + acc_scratch, 3 * work,
    )
    gain, tilted = call(
        partial(turn_kernel, plan=plan, count=count), "turn", tables,
        (gain, poly, dual, chan_sum(energy, chans), ohp, ohq, *state),
        [field, field], parts_scratch + acc_scratch, work,
    )
    *state, energy = call(
        partial(residual_kernel, plan=plan), "residual", (starts,), (gain, ohp, ohq, *msgs),
        keep + [tile], gather_scratch, work,
    )
    fields = chan_gather(tilted, chans)
    acc = call(
        partial(normal_kernel, plan=plan, count=count), "normal", (starts,),
        (chan_sum(energy, chans), ohp, ohq, *state), acc_shape, parts_scratch, work,
    )
    gain, dual, *state, energy = call(
        partial(resume_kernel, plan=plan), "resume", tables, (gain, fields, acc, ohp, ohq, *msgs),
        [field, field] + keep + [tile], gather_scratch, work,
    )
    pieces = call(
        partial(last_kernel, plan=plan, count=count), "last", tables,
        (gain, fields, dual, chan_sum(energy, chans), ohp, ohq, *state),
        [shape(2 * rows, own)] * (plan.centre + 1), parts_scratch + acc_scratch, work,
    )
    mine = pieces[0]
    for n, pairs_of in enumerate(plan.outward(), 1):
        got = lax.ppermute(pieces[n], "stn", pairs_of)
        away = jnp.where(z <= plan.centre, plan.centre - z, z - plan.mirror(plan.centre))
        mine = jnp.where(away == n, got, mine)
    gain, tilted = mine[:rows], mine[rows:]
    fit, dual = call(
        partial(final_kernel, plan=plan), "final", (basis, index), (chan_gather(tilted, chans),),
        [shape(TERMS, rows, own), shape(rows, own)], [], 1 << 24,
    )
    out = (1, COMPS, paths, own)
    return gain.reshape(out), dual.reshape(out), fit.reshape((TERMS,) + out[1:])


def solution(mesh):
    placed = (
        P("chan", None, "stn"),
        P("chan", None, None, "stn"),
        P(),
        P(None, "stn"),
        P("chan", None, None, None),
        P(),
        P("chan", None, None, None),
        P(),
    )
    return jax.shard_map(
        partial(body, chans=mesh.shape["chan"], blocks=mesh.shape["stn"]),
        mesh=mesh,
        in_specs=placed,
        out_specs=(
            P("chan", None, None, "stn"),
            P("chan", None, None, "stn"),
            P(None, None, None, "stn"),
        ),
        check_vma=False,
    )
```

time: 208 us -> 125 us (0.60)
  local copies, waits for them, and re-layouts: 53.4 us -> 8.92 us
  other arithmetic: 32.7 us -> 0.85 us
  starting transfers between devices: 21.8 us -> 39 us
  blocking collectives: 16.5 us -> 0 us
  between operations: 6.17 us -> 1 us
  waiting for transfers between devices: 41.3 us -> 37 us
  Pallas kernels: 33.7 us -> 37.8 us
    unnamed x94 -> x36, local copies, waits for them, and re-layouts: 46.6 us -> 8.28 us
    ppermute x3 -> x31, starting transfers between devices: 6.14 us -> 39 us  [the longest x16 15.6 us: chan_sum(): lax.ppermute(x, 'chan', partners(count, d * span))]
    all_to_all x4 -> x0, waiting for transfers between devices: 21.7 us -> none  [exchange(): lax.all_to_all(jnp.broadcast_to(array[None], (chans,) + array.shape), 'ch...]
    ppermute x3 -> x31, waiting for transfers between devices: 19.6 us -> 37 us  [the longest x16 12.2 us: chan_sum(): lax.ppermute(x, 'chan', partners(count, d * span))]
    all_to_all x2 -> x0, blocking collectives: 16.5 us -> none  [exchange(): lax.all_to_all(jnp.broadcast_to(array[None], (chans,) + array.shape), 'ch...]
    sub x3 -> x0, other arithmetic: 16 us -> none  [the longest x1 12.1 us: body(): dual_now = tilted - consensus]
    all_to_all x4 -> x0, starting transfers between devices: 15.7 us -> none  [exchange(): lax.all_to_all(jnp.broadcast_to(array[None], (chans,) + array.shape), 'ch...]
    another operation x5 -> x1, other arithmetic: 10.6 us -> 0.08 us  [body(): index = jnp.stack([me, z, outward]).astype(jnp.int32)]
  transfers between devices with their start and end apart: 7 -> 31, of which waited for: 6 -> 20; matrix products, arithmetic and copies ran while one was open for 5% -> 0% of each run, Pallas kernels for 0% -> 4%
where the time goes in v2:
time: 125 us
  starting transfers between devices  39 us (31%)
  Pallas kernels  37.8 us (30%)
  waiting for transfers between devices  37 us (30%)
  local copies, waits for them, and re-layouts  8.92 us (7%)
    pallas_call x9, Pallas kernels, call(): pl.pallas_call(kernel, out_shape=outs, in_specs=[SM] * len(smem) + [ANY i...  37.8 us
    ppermute x16, starting transfers between devices, chan_sum(): lax.ppermute(x, 'chan', partners(count, d * span))  15.6 us
    ppermute x16, waiting for transfers between devices, chan_sum(): lax.ppermute(x, 'chan', partners(count, d * span))  12.2 us
    ppermute x8, waiting for transfers between devices, chan_gather(): lax.ppermute(x, 'chan', partners(count, d * span))  10.9 us
    ppermute x3, waiting for transfers between devices, body(): lax.ppermute(energy, 'stn', pairs_of)  9 us
    ppermute x3, starting transfers between devices, body(): lax.ppermute(msg, 'stn', pairs_of)  8.74 us
    unnamed x36, local copies, waits for them, and re-layouts  8.28 us
    ppermute x8, starting transfers between devices, chan_gather(): lax.ppermute(x, 'chan', partners(count, d * span))  7.18 us
  transfers between devices with their start and end apart: 31, of which 20 were waited for; matrix products, arithmetic and copies ran while one was open for 0% of the time, Pallas kernels for 4%

profile of v2, /device:TPU:0, one launch (start us, length us, event | category | flops | bytes accessed | tf_op | source)
XLA Modules:
  0.0 124.6 jit_solution(15411994345147312154)
XLA Ops:
  1.3 1.0 copy-done
  2.4 0.8 copy-done.7
  4.5 1.1 combine.1.msg_ref.refs_0_
  5.6 0.9 copy-done.12
  6.5 1.2 local.1
  8.3 0.8 collective-permute-done
  9.2 3.8 %collective-permute-start.3 = (f32[8,128]{1,0:T(8,128)S(1)}, f32[8,128]{1,0:T(8,128)S(1)}, u32[]{:S(2)}, u32[]{:S(2)}) collective-permute-start(f32[8,128]{1,0:T(8,128)S(1)} %add.54), channel_id=1, source_target_pairs={{0,24},{4,28},{8,16},{12,20},{16,8},{20,12},{24,0},{28,4},{1,25},{... | collective-permute-start | bytes 12296 | tf_op jit(solution)/shard_map/ppermute | solution.py:133
  13.5 5.0 %collective-permute-start.9 = (f32[80,1024]{1,0:T(8,128)S(1)}, f32[80,1024]{1,0:T(8,128)S(1)}, u32[]{:S(2)}, u32[]{:S(2)}) collective-permute-start(f32[80,1024]{1,0:T(8,128)S(1)} %combine.1.msg_ref.refs_0_), channel_id=1, source_target_pairs={{3,1},{0,2},{7,5},{4,6},{11,9},{8,10},{15,13},{12,14},{19,17},{16,... | collective-permute-start | bytes 983048 | tf_op jit(solution)/shard_map/ppermute | solution.py:447
  19.2 3.1 %collective-permute-start.7 = (f32[80,1024]{1,0:T(8,128)S(1)}, f32[80,1024]{1,0:T(8,128)S(1)}, u32[]{:S(2)}, u32[]{:S(2)}) collective-permute-start(f32[80,1024]{1,0:T(8,128)S(1)} %combine.1.msg_ref.refs_0_), channel_id=1, source_target_pairs={{0,1},{3,2},{4,5},{7,6},{8,9},{11,10},{12,13},{15,14},{16,17},{19,... | collective-permute-start | bytes 983048 | tf_op jit(solution)/shard_map/ppermute | solution.py:447
  22.3 1.3 %collective-permute-start.6 = (f32[8,128]{1,0:T(8,128)S(1)}, f32[8,128]{1,0:T(8,128)S(1)}, u32[]{:S(2)}, u32[]{:S(2)}) collective-permute-start(f32[8,128]{1,0:T(8,128)S(1)} %add_add_fusion.3), channel_id=1, source_target_pairs={{3,1},{0,2},{7,5},{4,6},{11,9},{8,10},{15,13},{12,14},{19,17},{16,... | collective-permute-start | bytes 12296 | tf_op jit(solution)/shard_map/ppermute | solution.py:468
  24.3 7.8 %collective-permute-done.6 = f32[8,128]{1,0:T(8,128)S(1)} collective-permute-done((f32[8,128]{1,0:T(8,128)S(1)}, f32[8,128]{1,0:T(8,128)S(1)}, u32[]{:S(2)}, u32[]{:S(2)}) %collective-permute-start.6) | collective-permute-done | bytes 4128 | tf_op jit(solution)/shard_map/ppermute | solution.py:468
  32.1 4.3 %collective-permute-start.4 = (f32[8,128]{1,0:T(8,128)S(1)}, f32[8,128]{1,0:T(8,128)S(1)}, u32[]{:S(2)}, u32[]{:S(2)}) collective-permute-start(f32[8,128]{1,0:T(8,128)S(1)} %add_add_fusion.3), channel_id=1, source_target_pairs={{0,1},{3,2},{4,5},{7,6},{8,9},{11,10},{12,13},{15,14},{16,17},{19,... | collective-permute-start | bytes 12296 | tf_op jit(solution)/shard_map/ppermute | solution.py:468
  36.4 1.2 collective-permute-done.4
  37.7 1.0 copy-done.1
  38.7 0.9 copy-done.3
  41.0 0.9 copy-done.13
  41.9 11.9 %first.1 = (bf16[128,4096]{1,0:T(8,128)(2,1)S(1)}, bf16[512,4096]{1,0:T(8,128)(2,1)S(1)}, f32[64,512]{1,0:T(8,128)S(1)}, f32[64,4096]{1,0:T(8,128)S(1)}, f32[64,...) custom-call(f32[8]{0:T(128)S(1)} %copy-done.9, s32[4]{0:T(128)S(1)} %fusion.starts_ref, ...), custom_call_target="tpu_custom_call" | custom-call | flops 6442450944 | bytes 1048576 | tf_op jit(solution)/shard_map/first/pallas_call | solution.py:411
  53.9 1.2 collective-permute-done.10
  55.0 2.4 %collective-permute-start.13 = (f32[8,128]{1,0:T(8,128)S(1)}, f32[8,128]{1,0:T(8,128)S(1)}, u32[]{:S(2)}, u32[]{:S(2)}) collective-permute-start(f32[8,128]{1,0:T(8,128)S(1)} %add.58), channel_id=1, source_target_pairs={{0,24},{4,28},{8,16},{12,20},{16,8},{20,12},{24,0},{28,4},{1,25},{... | collective-permute-start | bytes 12296 | tf_op jit(solution)/shard_map/ppermute | solution.py:133
  58.5 1.0 collective-permute-done.13
  59.5 1.5 %collective-permute-done.12 = f32[8,128]{1,0:T(8,128)S(1)} collective-permute-done((f32[8,128]{1,0:T(8,128)S(1)}, f32[8,128]{1,0:T(8,128)S(1)}, u32[]{:S(2)}, u32[]{:S(2)}) %collective-permute-start.12) | collective-permute-done | bytes 4128 | tf_op jit(solution)/shard_map/ppermute | solution.py:133
  61.6 4.8 %turn.1 = (f32[64,512]{1,0:T(8,128)S(1)}, f32[64,512]{1,0:T(8,128)S(1)}) custom-call(f32[8]{0:T(128)S(1)} %copy-done.10, s32[4]{0:T(128)S(1)} %fusion.starts_ref, f32[8,3]{1,0:T(8,128)S(1)} %copy-done.6, s32[3]{0:T(128)S(1)} %pad_add_fusion.index_ref, f32[64,512]{1,0:T(8,128)S(1)} %get-tuple-element.29.gain_ref, f32[3,64,512]{2,1,0:T(8,128)S(1)} %bitcast.33, ...), custom_call_target="tpu_custom_call" | custom-call | flops 2147483648 | bytes 1048576 | tf_op jit(solution)/shard_map/turn/pallas_call | solution.py:411
  66.5 3.5 %residual.1 = (f32[64,4096]{1,0:T(8,128)S(1)}, f32[64,4096]{1,0:T(8,128)S(1)}, f32[64,4096]{1,0:T(8,128)S(1)}, f32[8,4096]{1,0:T(8,128)S(1)}, f32[8,128]{1,0:T(8,128)S(1)}) custom-call(s32[4]{0:T(128)S(1)} %fusion.starts_ref, f32[64,512]{1,0:T(8,128)S(1)} %get-tuple-element.37.gain_ref, bf16[128,4096]{1,0:T(8,128)(2,1)S(1)} %get-tuple-element.31.ohp_ref, ...), custom_call_target="tpu_custom_call" | custom-call | flops 2147483648 | bytes 1048576 | tf_op jit(solution)/shard_map/residual/pallas_call | solution.py:411
  70.1 1.2 collective-permute-done.18
  71.2 1.5 %collective-permute-start.21 = (f32[8,128]{1,0:T(8,128)S(1)}, f32[8,128]{1,0:T(8,128)S(1)}, u32[]{:S(2)}, u32[]{:S(2)}) collective-permute-start(f32[8,128]{1,0:T(8,128)S(1)} %add.62), channel_id=1, source_target_pairs={{0,24},{4,28},{8,16},{12,20},{16,8},{20,12},{24,0},{28,4},{1,25},{... | collective-permute-start | bytes 12296 | tf_op jit(solution)/shard_map/ppermute | solution.py:133
  73.2 1.5 %collective-permute-start.19 = (f32[8,128]{1,0:T(8,128)S(1)}, f32[8,128]{1,0:T(8,128)S(1)}, u32[]{:S(2)}, u32[]{:S(2)}) collective-permute-start(f32[8,128]{1,0:T(8,128)S(1)} %add.62), channel_id=1, source_target_pairs={{0,8},{4,12},{8,0},{12,4},{16,24},{20,28},{24,16},{28,20},{1,9},{5... | collective-permute-start | bytes 12296 | tf_op jit(solution)/shard_map/ppermute | solution.py:133
  74.8 0.9 collective-permute-done.21
  76.9 1.6 %collective-permute-start.16 = (f32[2,64,512]{2,1,0:T(8,128)S(1)}, f32[2,64,512]{2,1,0:T(8,128)S(1)}, u32[]{:S(2)}, u32[]{:S(2)}) collective-permute-start(f32[2,64,512]{2,1,0:T(8,128)S(1)} %pad_maximum_fusion), channel_id=1, source_target_pairs={{0,16},{4,20},{8,24},{12,28},{16,0},{20,4},{24,8},{28,12},{1,17},{... | collective-permute-start | bytes 786440 | tf_op jit(solution)/shard_map/ppermute | solution.py:144
  78.4 1.5 %collective-permute-start.15 = (f32[2,64,512]{2,1,0:T(8,128)S(1)}, f32[2,64,512]{2,1,0:T(8,128)S(1)}, u32[]{:S(2)}, u32[]{:S(2)}) collective-permute-start(f32[2,64,512]{2,1,0:T(8,128)S(1)} %pad_maximum_fusion), channel_id=1, source_target_pairs={{0,8},{4,12},{8,0},{12,4},{16,24},{20,28},{24,16},{28,20},{1,9},{5... | collective-permute-start | bytes 786440 | tf_op jit(solution)/shard_map/ppermute | solution.py:144
  79.9 4.7 %normal.1.acc_ref = f32[96,512]{1,0:T(8,128)S(1)} custom-call(s32[4]{0:T(128)S(1)} %fusion.starts_ref, f32[8,128]{1,0:T(8,128)S(1)} %add_add_fusion.1.energy_ref, bf16[128,4096]{1,0:T(8,128)(2,1)S(1)} %get-tuple-element.31.ohp_ref, bf16[512,4096]{1,0:T(8,128)(2,1)S(1)} %get-tuple-element.32.ohq_ref, f32[64,4096]{1,0:T(8,128)S(1)} %get-tuple-element.40.refs_0_, ...), custom_call_target="tpu_custom_call" | custom-call | flops 2147483648 | bytes 1048576 | tf_op jit(solution)/shard_map/normal/pallas_call | solution.py:411
  85.2 1.3 %collective-permute-done.15 = f32[2,64,512]{2,1,0:T(8,128)S(1)} collective-permute-done((f32[2,64,512]{2,1,0:T(8,128)S(1)}, f32[2,64,512]{2,1,0:T(8,128)S(1)}, u32[]{:S(2)}, u32[]{:S(2)}) %collective-permute-start.15) | collective-permute-done | bytes 262176 | tf_op jit(solution)/shard_map/ppermute | solution.py:144
  86.5 5.4 %collective-permute-done.17 = f32[2,64,512]{2,1,0:T(8,128)S(1)} collective-permute-done((f32[2,64,512]{2,1,0:T(8,128)S(1)}, f32[2,64,512]{2,1,0:T(8,128)S(1)}, u32[]{:S(2)}, u32[]{:S(2)}) %collective-permute-start.17) | collective-permute-done | bytes 262176 | tf_op jit(solution)/shard_map/ppermute | solution.py:144
  92.0 4.1 %resume.1 = (f32[64,512]{1,0:T(8,128)S(1)}, f32[64,512]{1,0:T(8,128)S(1)}, f32[64,4096]{1,0:T(8,128)S(1)}, f32[64,4096]{1,0:T(8,128)S(1)}, f32[64,4096]{1,0:T(8,...) custom-call(f32[8]{0:T(128)S(1)} %copy-done.10, s32[4]{0:T(128)S(1)} %fusion.starts_ref, f32[8,3]{1,0:T(8,128)S(1)} %copy-done.6, ...), custom_call_target="tpu_custom_call" | custom-call | flops 2147483648 | bytes 1048576 | tf_op jit(solution)/shard_map/resume/pallas_call | solution.py:411
  96.2 1.2 collective-permute-done.22
  97.3 1.2 collective-permute-start.25
  98.5 1.5 %collective-permute-start.24 = (f32[8,128]{1,0:T(8,128)S(1)}, f32[8,128]{1,0:T(8,128)S(1)}, u32[]{:S(2)}, u32[]{:S(2)}) collective-permute-start(f32[8,128]{1,0:T(8,128)S(1)} %add.66), channel_id=1, source_target_pairs={{0,16},{4,20},{8,24},{12,28},{16,0},{20,4},{24,8},{28,12},{1,17},{... | collective-permute-start | bytes 12296 | tf_op jit(solution)/shard_map/ppermute | solution.py:133
  100.0 0.8 collective-permute-start.23
  100.8 1.0 collective-permute-done.25
  102.1 1.5 %collective-permute-done.23 = f32[8,128]{1,0:T(8,128)S(1)} collective-permute-done((f32[8,128]{1,0:T(8,128)S(1)}, f32[8,128]{1,0:T(8,128)S(1)}, u32[]{:S(2)}, u32[]{:S(2)}) %collective-permute-start.23) | collective-permute-done | bytes 4128 | tf_op jit(solution)/shard_map/ppermute | solution.py:133
  103.6 5.1 %last.1 = (f32[128,128]{1,0:T(8,128)S(1)}, f32[128,128]{1,0:T(8,128)S(1)}) custom-call(f32[8]{0:T(128)S(1)} %copy-done.10, s32[4]{0:T(128)S(1)} %fusion.starts_ref, f32[8,3]{1,0:T(8,128)S(1)} %copy-done.6, s32[3]{0:T(128)S(1)} %pad_add_fusion.index_ref, f32[64,512]{1,0:T(8,128)S(1)} %get-tuple-element.44.gain_ref, ...), custom_call_target="tpu_custom_call" | custom-call | flops 2147483648 | bytes 1048576 | tf_op jit(solution)/shard_map/last/pallas_call | solution.py:411
  108.8 1.3 %collective-permute-start.26 = (f32[128,128]{1,0:T(8,128)S(1)}, f32[128,128]{1,0:T(8,128)S(1)}, u32[]{:S(2)}, u32[]{:S(2)}) collective-permute-start(f32[128,128]{1,0:T(8,128)S(1)} %get-tuple-element.51), channel_id=1, source_target_pairs={{1,0},{2,3},{5,4},{6,7},{9,8},{10,11},{13,12},{14,15},{17,16},{18,... | collective-permute-start | bytes 196616 | tf_op jit(solution)/shard_map/ppermute | solution.py:502
  110.1 4.8 %collective-permute-done.26 = f32[128,128]{1,0:T(8,128)S(1)} collective-permute-done((f32[128,128]{1,0:T(8,128)S(1)}, f32[128,128]{1,0:T(8,128)S(1)}, u32[]{:S(2)}, u32[]{:S(2)}) %collective-permute-start.26) | collective-permute-done | bytes 65568 | tf_op jit(solution)/shard_map/ppermute | solution.py:502
  115.6 1.2 collective-permute-done.27
  116.8 1.1 collective-permute-start.30
  117.9 1.1 collective-permute-start.29
  119.0 1.3 %collective-permute-start.28 = (f32[2,64,128]{2,1,0:T(8,128)S(1)}, f32[2,64,128]{2,1,0:T(8,128)S(1)}, u32[]{:S(2)}, u32[]{:S(2)}) collective-permute-start(f32[2,64,128]{2,1,0:T(8,128)S(1)} %pad_maximum_fusion.1), channel_id=1, source_target_pairs={{0,8},{4,12},{8,0},{12,4},{16,24},{20,28},{24,16},{28,20},{1,9},{5... | collective-permute-start | bytes 196616 | tf_op jit(solution)/shard_map/ppermute | solution.py:144
  120.3 3.0 %collective-permute-done.28 = f32[2,64,128]{2,1,0:T(8,128)S(1)} collective-permute-done((f32[2,64,128]{2,1,0:T(8,128)S(1)}, f32[2,64,128]{2,1,0:T(8,128)S(1)}, u32[]{:S(2)}, u32[]{:S(2)}) %collective-permute-start.28) | collective-permute-done | bytes 65568 | tf_op jit(solution)/shard_map/ppermute | solution.py:144
  123.3 1.3 %final.1 = (f32[3,64,128]{2,1,0:T(8,128)}, f32[64,128]{1,0:T(8,128)}) custom-call(f32[8,3]{1,0:T(8,128)S(1)} %copy-done.6, s32[3]{0:T(128)S(1)} %pad_add_fusion.index_ref, f32[8,64,128]{2,1,0:T(8,128)S(1)} %constant_dynamic-update-slice_fusion.5.field_ref), custom_call_target="tpu_custom_call" | custom-call | flops 16777216 | bytes 1048576 | tf_op jit(solution)/shard_map/final/pallas_call | solution.py:411
  (76 shorter events, 11.1 us)
Async XLA Ops:
  1.3 1.0 copy-start
  2.4 0.8 copy-start.7
  3.1 0.7 copy-start.8
  3.8 0.7 copy-start.11
  5.6 0.9 copy-start.12
  7.8 1.4 %collective-permute-start = (f32[8,128]{1,0:T(8,128)S(1)}, f32[8,128]{1,0:T(8,128)S(1)}, u32[]{:S(2)}, u32[]{:S(2)}) collective-permute-start(f32[8,128]{1,0:T(8,128)S(1)} %local.1), channel_id=1, source_target_pairs={{0,4},{4,0},{8,12},{12,8},{16,20},{20,16},{24,28},{28,24},{1,5},{5... | collective-permute-start | bytes 12296 | tf_op jit(solution)/shard_map/ppermute | solution.py:133
  9.2 10.0 %collective-permute-start.3 = (f32[8,128]{1,0:T(8,128)S(1)}, f32[8,128]{1,0:T(8,128)S(1)}, u32[]{:S(2)}, u32[]{:S(2)}) collective-permute-start(f32[8,128]{1,0:T(8,128)S(1)} %add.54), channel_id=1, source_target_pairs={{0,24},{4,28},{8,16},{12,20},{16,8},{20,12},{24,0},{28,4},{1,25},{... | collective-permute-start | bytes 12296 | tf_op jit(solution)/shard_map/ppermute | solution.py:133
  12.9 9.3 %collective-permute-start.2 = (f32[8,128]{1,0:T(8,128)S(1)}, f32[8,128]{1,0:T(8,128)S(1)}, u32[]{:S(2)}, u32[]{:S(2)}) collective-permute-start(f32[8,128]{1,0:T(8,128)S(1)} %add.54), channel_id=1, source_target_pairs={{0,16},{4,20},{8,24},{12,28},{16,0},{20,4},{24,8},{28,12},{1,17},{... | collective-permute-start | bytes 12296 | tf_op jit(solution)/shard_map/ppermute | solution.py:133
  13.4 8.8 %collective-permute-start.1 = (f32[8,128]{1,0:T(8,128)S(1)}, f32[8,128]{1,0:T(8,128)S(1)}, u32[]{:S(2)}, u32[]{:S(2)}) collective-permute-start(f32[8,128]{1,0:T(8,128)S(1)} %add.54), channel_id=1, source_target_pairs={{0,8},{4,12},{8,0},{12,4},{16,24},{20,28},{24,16},{28,20},{1,9},{5... | collective-permute-start | bytes 12296 | tf_op jit(solution)/shard_map/ppermute | solution.py:133
  13.5 24.2 %collective-permute-start.9 = (f32[80,1024]{1,0:T(8,128)S(1)}, f32[80,1024]{1,0:T(8,128)S(1)}, u32[]{:S(2)}, u32[]{:S(2)}) collective-permute-start(f32[80,1024]{1,0:T(8,128)S(1)} %combine.1.msg_ref.refs_0_), channel_id=1, source_target_pairs={{3,1},{0,2},{7,5},{4,6},{11,9},{8,10},{15,13},{12,14},{19,17},{16,... | collective-permute-start | bytes 983048 | tf_op jit(solution)/shard_map/ppermute | solution.py:447
  18.5 19.2 %collective-permute-start.8 = (f32[80,1024]{1,0:T(8,128)S(1)}, f32[80,1024]{1,0:T(8,128)S(1)}, u32[]{:S(2)}, u32[]{:S(2)}) collective-permute-start(f32[80,1024]{1,0:T(8,128)S(1)} %combine.1.msg_ref.refs_0_), channel_id=1, source_target_pairs={{2,1},{1,2},{6,5},{5,6},{10,9},{9,10},{14,13},{13,14},{18,17},{17,... | collective-permute-start | bytes 983048 | tf_op jit(solution)/shard_map/ppermute | solution.py:447
  19.2 18.5 %collective-permute-start.7 = (f32[80,1024]{1,0:T(8,128)S(1)}, f32[80,1024]{1,0:T(8,128)S(1)}, u32[]{:S(2)}, u32[]{:S(2)}) collective-permute-start(f32[80,1024]{1,0:T(8,128)S(1)} %combine.1.msg_ref.refs_0_), channel_id=1, source_target_pairs={{0,1},{3,2},{4,5},{7,6},{8,9},{11,10},{12,13},{15,14},{16,17},{19,... | collective-permute-start | bytes 983048 | tf_op jit(solution)/shard_map/ppermute | solution.py:447
  22.3 9.8 %collective-permute-start.6 = (f32[8,128]{1,0:T(8,128)S(1)}, f32[8,128]{1,0:T(8,128)S(1)}, u32[]{:S(2)}, u32[]{:S(2)}) collective-permute-start(f32[8,128]{1,0:T(8,128)S(1)} %add_add_fusion.3), channel_id=1, source_target_pairs={{3,1},{0,2},{7,5},{4,6},{11,9},{8,10},{15,13},{12,14},{19,17},{16,... | collective-permute-start | bytes 12296 | tf_op jit(solution)/shard_map/ppermute | solution.py:468
  23.6 12.8 %collective-permute-start.5 = (f32[8,128]{1,0:T(8,128)S(1)}, f32[8,128]{1,0:T(8,128)S(1)}, u32[]{:S(2)}, u32[]{:S(2)}) collective-permute-start(f32[8,128]{1,0:T(8,128)S(1)} %add_add_fusion.3), channel_id=1, source_target_pairs={{2,1},{1,2},{6,5},{5,6},{10,9},{9,10},{14,13},{13,14},{18,17},{17,... | collective-permute-start | bytes 12296 | tf_op jit(solution)/shard_map/ppermute | solution.py:468
  32.1 5.6 %collective-permute-start.4 = (f32[8,128]{1,0:T(8,128)S(1)}, f32[8,128]{1,0:T(8,128)S(1)}, u32[]{:S(2)}, u32[]{:S(2)}) collective-permute-start(f32[8,128]{1,0:T(8,128)S(1)} %add_add_fusion.3), channel_id=1, source_target_pairs={{0,1},{3,2},{4,5},{7,6},{8,9},{11,10},{12,13},{15,14},{16,17},{19,... | collective-permute-start | bytes 12296 | tf_op jit(solution)/shard_map/ppermute | solution.py:468
  37.7 1.0 copy-start.1
  38.7 0.9 copy-start.3
  39.6 0.7 copy-start.5
  40.3 0.7 copy-start.9
  40.9 0.9 copy-start.13
  41.9 19.7 %copy-start.2 = (f32[3,8,8,512]{3,2,1,0:T(8,128)S(1)}, f32[3,8,8,512]{3,2,1,0:T(8,128)}, u32[]{:S(2)}) copy-start(f32[3,8,8,512]{3,2,1,0:T(8,128)} %param.15) | copy-start | bytes 1179652
  41.9 19.7 %copy-start.4 = (f32[1,8,8,512]{3,2,1,0:T(8,128)S(1)}, f32[1,8,8,512]{3,2,1,0:T(8,128)}, u32[]{:S(2)}) copy-start(f32[1,8,8,512]{3,2,1,0:T(8,128)} %param.16) | copy-start | bytes 393220
  41.9 19.7 %copy-start.6 = (f32[8,3]{1,0:T(8,128)S(1)}, f32[8,3]{1,0:T(8,128)}, u32[]{:S(2)}) copy-start(f32[8,3]{1,0:T(8,128)} %constant.39.clone.basis_ref) | copy-start | bytes 292
  41.9 19.7 %copy-start.10 = (f32[8]{0:T(128)S(1)}, f32[8]{0:T(128)}, u32[]{:S(2)}) copy-start(f32[8]{0:T(128)} %rho_ref.7) | copy-start | bytes 100
  53.8 1.2 collective-permute-start.10
  55.0 4.5 %collective-permute-start.13 = (f32[8,128]{1,0:T(8,128)S(1)}, f32[8,128]{1,0:T(8,128)S(1)}, u32[]{:S(2)}, u32[]{:S(2)}) collective-permute-start(f32[8,128]{1,0:T(8,128)S(1)} %add.58), channel_id=1, source_target_pairs={{0,24},{4,28},{8,16},{12,20},{16,8},{20,12},{24,0},{28,4},{1,25},{... | collective-permute-start | bytes 12296 | tf_op jit(solution)/shard_map/ppermute | solution.py:133
  57.5 3.6 %collective-permute-start.12 = (f32[8,128]{1,0:T(8,128)S(1)}, f32[8,128]{1,0:T(8,128)S(1)}, u32[]{:S(2)}, u32[]{:S(2)}) collective-permute-start(f32[8,128]{1,0:T(8,128)S(1)} %add.58), channel_id=1, source_target_pairs={{0,16},{4,20},{8,24},{12,28},{16,0},{20,4},{24,8},{28,12},{1,17},{... | collective-permute-start | bytes 12296 | tf_op jit(solution)/shard_map/ppermute | solution.py:133
  58.0 3.6 %collective-permute-start.11 = (f32[8,128]{1,0:T(8,128)S(1)}, f32[8,128]{1,0:T(8,128)S(1)}, u32[]{:S(2)}, u32[]{:S(2)}) collective-permute-start(f32[8,128]{1,0:T(8,128)S(1)} %add.58), channel_id=1, source_target_pairs={{0,8},{4,12},{8,0},{12,4},{16,24},{20,28},{24,16},{28,20},{1,9},{5... | collective-permute-start | bytes 12296 | tf_op jit(solution)/shard_map/ppermute | solution.py:133
  70.0 1.2 collective-permute-start.18
  71.2 4.5 %collective-permute-start.21 = (f32[8,128]{1,0:T(8,128)S(1)}, f32[8,128]{1,0:T(8,128)S(1)}, u32[]{:S(2)}, u32[]{:S(2)}) collective-permute-start(f32[8,128]{1,0:T(8,128)S(1)} %add.62), channel_id=1, source_target_pairs={{0,24},{4,28},{8,16},{12,20},{16,8},{20,12},{24,0},{28,4},{1,25},{... | collective-permute-start | bytes 12296 | tf_op jit(solution)/shard_map/ppermute | solution.py:133
  72.7 3.6 %collective-permute-start.20 = (f32[8,128]{1,0:T(8,128)S(1)}, f32[8,128]{1,0:T(8,128)S(1)}, u32[]{:S(2)}, u32[]{:S(2)}) collective-permute-start(f32[8,128]{1,0:T(8,128)S(1)} %add.62), channel_id=1, source_target_pairs={{0,16},{4,20},{8,24},{12,28},{16,0},{20,4},{24,8},{28,12},{1,17},{... | collective-permute-start | bytes 12296 | tf_op jit(solution)/shard_map/ppermute | solution.py:133
  73.2 3.6 %collective-permute-start.19 = (f32[8,128]{1,0:T(8,128)S(1)}, f32[8,128]{1,0:T(8,128)S(1)}, u32[]{:S(2)}, u32[]{:S(2)}) collective-permute-start(f32[8,128]{1,0:T(8,128)S(1)} %add.62), channel_id=1, source_target_pairs={{0,8},{4,12},{8,0},{12,4},{16,24},{20,28},{24,16},{28,20},{1,9},{5... | collective-permute-start | bytes 12296 | tf_op jit(solution)/shard_map/ppermute | solution.py:133
  74.7 2.1 %collective-permute-start.14 = (f32[1,64,512]{2,1,0:T(8,128)S(1)}, f32[1,64,512]{2,1,0:T(8,128)S(1)}, u32[]{:S(2)}, u32[]{:S(2)}) collective-permute-start(f32[1,64,512]{2,1,0:T(8,128)S(1)} %bitcast.30), channel_id=1, source_target_pairs={{0,4},{4,0},{8,12},{12,8},{16,20},{20,16},{24,28},{28,24},{1,5},{5... | collective-permute-start | bytes 393224 | tf_op jit(solution)/shard_map/ppermute | solution.py:144
  76.9 9.6 %collective-permute-start.16 = (f32[2,64,512]{2,1,0:T(8,128)S(1)}, f32[2,64,512]{2,1,0:T(8,128)S(1)}, u32[]{:S(2)}, u32[]{:S(2)}) collective-permute-start(f32[2,64,512]{2,1,0:T(8,128)S(1)} %pad_maximum_fusion), channel_id=1, source_target_pairs={{0,16},{4,20},{8,24},{12,28},{16,0},{20,4},{24,8},{28,12},{1,17},{... | collective-permute-start | bytes 786440 | tf_op jit(solution)/shard_map/ppermute | solution.py:144
  78.4 8.0 %collective-permute-start.15 = (f32[2,64,512]{2,1,0:T(8,128)S(1)}, f32[2,64,512]{2,1,0:T(8,128)S(1)}, u32[]{:S(2)}, u32[]{:S(2)}) collective-permute-start(f32[2,64,512]{2,1,0:T(8,128)S(1)} %pad_maximum_fusion), channel_id=1, source_target_pairs={{0,8},{4,12},{8,0},{12,4},{16,24},{20,28},{24,16},{28,20},{1,9},{5... | collective-permute-start | bytes 786440 | tf_op jit(solution)/shard_map/ppermute | solution.py:144
  84.6 7.3 %collective-permute-start.17 = (f32[2,64,512]{2,1,0:T(8,128)S(1)}, f32[2,64,512]{2,1,0:T(8,128)S(1)}, u32[]{:S(2)}, u32[]{:S(2)}) collective-permute-start(f32[2,64,512]{2,1,0:T(8,128)S(1)} %pad_maximum_fusion), channel_id=1, source_target_pairs={{0,24},{4,28},{8,16},{12,20},{16,8},{20,12},{24,0},{28,4},{1,25},{... | collective-permute-start | bytes 786440 | tf_op jit(solution)/shard_map/ppermute | solution.py:144
  96.1 1.2 collective-permute-start.22
  97.3 4.5 %collective-permute-start.25 = (f32[8,128]{1,0:T(8,128)S(1)}, f32[8,128]{1,0:T(8,128)S(1)}, u32[]{:S(2)}, u32[]{:S(2)}) collective-permute-start(f32[8,128]{1,0:T(8,128)S(1)} %add.66), channel_id=1, source_target_pairs={{0,24},{4,28},{8,16},{12,20},{16,8},{20,12},{24,0},{28,4},{1,25},{... | collective-permute-start | bytes 12296 | tf_op jit(solution)/shard_map/ppermute | solution.py:133
  98.5 3.6 %collective-permute-start.24 = (f32[8,128]{1,0:T(8,128)S(1)}, f32[8,128]{1,0:T(8,128)S(1)}, u32[]{:S(2)}, u32[]{:S(2)}) collective-permute-start(f32[8,128]{1,0:T(8,128)S(1)} %add.66), channel_id=1, source_target_pairs={{0,16},{4,20},{8,24},{12,28},{16,0},{20,4},{24,8},{28,12},{1,17},{... | collective-permute-start | bytes 12296 | tf_op jit(solution)/shard_map/ppermute | solution.py:133
  100.0 3.6 %collective-permute-start.23 = (f32[8,128]{1,0:T(8,128)S(1)}, f32[8,128]{1,0:T(8,128)S(1)}, u32[]{:S(2)}, u32[]{:S(2)}) collective-permute-start(f32[8,128]{1,0:T(8,128)S(1)} %add.66), channel_id=1, source_target_pairs={{0,8},{4,12},{8,0},{12,4},{16,24},{20,28},{24,16},{28,20},{1,9},{5... | collective-permute-start | bytes 12296 | tf_op jit(solution)/shard_map/ppermute | solution.py:133
  108.8 6.2 %collective-permute-start.26 = (f32[128,128]{1,0:T(8,128)S(1)}, f32[128,128]{1,0:T(8,128)S(1)}, u32[]{:S(2)}, u32[]{:S(2)}) collective-permute-start(f32[128,128]{1,0:T(8,128)S(1)} %get-tuple-element.51), channel_id=1, source_target_pairs={{1,0},{2,3},{5,4},{6,7},{9,8},{10,11},{13,12},{14,15},{17,16},{18,... | collective-permute-start | bytes 196616 | tf_op jit(solution)/shard_map/ppermute | solution.py:502
  115.5 1.2 collective-permute-start.27
  116.8 6.5 %collective-permute-start.30 = (f32[2,64,128]{2,1,0:T(8,128)S(1)}, f32[2,64,128]{2,1,0:T(8,128)S(1)}, u32[]{:S(2)}, u32[]{:S(2)}) collective-permute-start(f32[2,64,128]{2,1,0:T(8,128)S(1)} %pad_maximum_fusion.1), channel_id=1, source_target_pairs={{0,24},{4,28},{8,16},{12,20},{16,8},{20,12},{24,0},{28,4},{1,25},{... | collective-permute-start | bytes 196616 | tf_op jit(solution)/shard_map/ppermute | solution.py:144
  117.9 5.4 %collective-permute-start.29 = (f32[2,64,128]{2,1,0:T(8,128)S(1)}, f32[2,64,128]{2,1,0:T(8,128)S(1)}, u32[]{:S(2)}, u32[]{:S(2)}) collective-permute-start(f32[2,64,128]{2,1,0:T(8,128)S(1)} %pad_maximum_fusion.1), channel_id=1, source_target_pairs={{0,16},{4,20},{8,24},{12,28},{16,0},{20,4},{24,8},{28,12},{1,17},{... | collective-permute-start | bytes 196616 | tf_op jit(solution)/shard_map/ppermute | solution.py:144
  119.0 4.3 %collective-permute-start.28 = (f32[2,64,128]{2,1,0:T(8,128)S(1)}, f32[2,64,128]{2,1,0:T(8,128)S(1)}, u32[]{:S(2)}, u32[]{:S(2)}) collective-permute-start(f32[2,64,128]{2,1,0:T(8,128)S(1)} %pad_maximum_fusion.1), channel_id=1, source_target_pairs={{0,8},{4,12},{8,0},{12,4},{16,24},{20,28},{24,16},{28,20},{1,9},{5... | collective-permute-start | bytes 196616 | tf_op jit(solution)/shard_map/ppermute | solution.py:144
